TPU v7x, 512 devices: a whole 4x4x16 slice. The times are simulated.
512 devices in a mesh: blk: 32 (over x, y, z_hi), rep: 16 (over z_lo, core).
Axes of the slice: x: 4, y: 4, z: 16 (z_hi: 2, z_lo: 8; z = z_hi * 8 + z_lo), core: 2. Of those that a mesh axis runs over, the one named last changes fastest.
Arguments:
- coords: float32 [192, 65536], P('rep', 'blk'), may hold values from -4 to 4
- eigvecs: float32 [128, 65536], P(None, ('blk', 'rep')), may hold values from -0.36 to 0.36
- nbr_list: int32 [512, 128], P('blk'), may hold values from 0 to 511, as said below
- nbr_count: int32 [512], P('blk'), may hold values from 32 to 128, as said below
Outputs:
- smoothed: float32 [128, 65536], P(None, ('blk', 'rep'))
Inputs may be any that keep to these rules, and one draw needn't show every extreme that they name: `nbr_count`: the largest count is exactly 128 in every draw; counts differ from block to block. `nbr_list`: the first nbr_count entries of a row are distinct block indices; entries after them are not used.
All inputs are finite; a program needn't handle non-finite values.
Results may differ from a plain program's by a relative error of at most 0.0003.
Values sent between devices are 32-bit elements; how exact they have to be, the bound alone decides.
A program may use at most 64 MiB of HBM per device.

v0:
```python
import jax
import jax.numpy as jnp
from jax import lax
from jax.sharding import PartitionSpec as P


def from_behind(value, axis, steps):
    count = lax.axis_size(axis)
    pairs = [(source, (source + steps) % count) for source in range(count)]
    return lax.ppermute(value, axis, pairs)


def shards(coords, eigvecs, nbr_list, nbr_count):
    cycle_size = lax.axis_size("blk")
    rep_size = lax.axis_size("rep")
    blk_index = lax.axis_index("blk")
    rep_index = lax.axis_index("rep")
    gathered = lax.all_gather(coords, "rep", axis=0, tiled=True)
    feat_count, group_width = gathered.shape
    group_blocks, slot_count = nbr_list.shape
    block_width = group_width // group_blocks
    eig_count, own_width = eigvecs.shape
    per_device = own_width // block_width
    kernel_scale = feat_count * 1.0
    batch_rows = 4
    row_tiles = gathered.reshape(feat_count, group_blocks, block_width)
    row_norms = jnp.sum(row_tiles * row_tiles, axis=0)
    owner_dev = nbr_list // per_device
    source_blk = owner_dev // rep_size
    source_rep = owner_dev % rep_size
    local_column = nbr_list % per_device
    slot_ids = jnp.arange(slot_count, dtype=jnp.int32)
    usable = (slot_ids[None, :] < nbr_count[:, None]) & (source_rep == rep_index)
    distance = (blk_index - source_blk) % cycle_size
    key_count = cycle_size * per_device
    slot_keys = jnp.where(usable, distance * per_device + local_column, key_count).reshape(-1)
    ordering = jnp.argsort(slot_keys, stable=True)
    sorted_keys = slot_keys[ordering]
    sorted_rows = jnp.concatenate([ordering // slot_count, jnp.zeros((batch_rows,), jnp.int32)])
    starts = jnp.searchsorted(sorted_keys, jnp.arange(key_count + 1, dtype=jnp.int32))

    def run_key(slot_key, col_coords, col_vecs, totals):
        first_slot = starts[slot_key]
        live_count = starts[slot_key + 1] - first_slot
        group_total = (live_count + batch_rows - 1) // batch_rows
        col_norms = jnp.sum(col_coords * col_coords, axis=0)

        def keep_going(state):
            return state[0] < group_total

        def one_group(state):
            done_groups, running = state
            first_pick = done_groups * batch_rows
            picked = lax.dynamic_slice_in_dim(sorted_rows, first_slot + first_pick, batch_rows)
            live_mask = first_pick + jnp.arange(batch_rows, dtype=jnp.int32) < live_count
            row_block = jnp.take(row_tiles, picked, axis=1)
            row_sq = jnp.take(row_norms, picked, axis=0)
            inner_prod = jnp.einsum(
                "fgt,fu->gtu", row_block, col_coords, precision=lax.Precision.HIGHEST
            )
            dist_sq = row_sq[:, :, None] + col_norms[None, None, :] - 2.0 * inner_prod
            weight = jnp.where(live_mask[:, None, None], jnp.exp(-dist_sq / kernel_scale), 0.0)
            contrib = jnp.einsum("gtu,eu->egt", weight, col_vecs, precision=lax.Precision.HIGHEST)
            return (done_groups + 1, running.at[:, picked, :].add(contrib))

        return lax.while_loop(keep_going, one_group, (jnp.int32(0), totals))[1]

    def use_panel(distance_now, panel, totals):
        col_coords = panel[:feat_count, 0:block_width]
        col_vecs = panel[feat_count:, 0:block_width]
        totals = run_key(distance_now * per_device + 0, col_coords, col_vecs, totals)
        return totals

    own_coords = lax.dynamic_slice_in_dim(gathered, rep_index * own_width, own_width, 1)
    panel = jnp.concatenate([own_coords, eigvecs], axis=0)
    totals = jnp.zeros((eig_count, group_blocks, block_width), jnp.float32)
    totals = use_panel(jnp.int32(0), panel, totals)

    def onward_turn(step_no, state):
        moving, running = state
        moving = from_behind(moving, "blk", 1)
        return (moving, use_panel(step_no, moving, running))

    totals = lax.fori_loop(1, cycle_size, onward_turn, (panel, totals))[1]
    partial_value = totals.reshape(eig_count, group_blocks * block_width)
    return lax.psum_scatter(partial_value, "rep", scatter_dimension=1, tiled=True)


def solution(mesh):
    return jax.shard_map(
        shards,
        mesh=mesh,
        in_specs=(P("rep", "blk"), P(None, ("blk", "rep")), P("blk", None), P("blk")),
        out_specs=P(None, ("blk", "rep")),
        check_vma=False,
    )
```

profile of v0, /device:TPU:6, one launch (start us, length us, event | category | flops | bytes accessed | tf_op | source)
XLA Modules:
  0.0 1129.9 jit_solution(2607958871408142795)
XLA Ops:
  8.1 5.0 sort.17
  13.2 11.8 %gather_fusion.5 = s32[2048]{0:T(1024)S(1)} fusion(s32[2048]{0:T(1024)S(1)} %fusion.32, s32[2048]{0:T(1024)S(1)} %get-tuple-element.676), kind=kCustom, calls=%fused_computation.5 | custom fusion | bytes 24576 | tf_op jit(solution)/shard_map/gather | solution.py:38
  24.9 9.9 while.96
  36.7 77.7 %all-gather.3.cloned.1.call-done = f32[16,12,2048]{2,1,0:T(8,128)} async-done(((f32[1,12,2048]{2,1,0:T(8,128)}), f32[16,12,2048]{2,1,0:T(8,128)}) %all-gather.3.cloned.1.call-update) | async-done | bytes 1572880 | tf_op jit(solution)/shard_map/all_gather | solution.py:18
  127.4 826.4 %while.95 = (s32[]{:T(128)}, f32[320,128]{1,0:T(8,128)S(1)}, f32[128,16,128]{2,0,1:T(8,128)S(1)}, s32[33]{0:T(128)S(1)}, s32[2052]{0:T(1024)S(1)}, /*index=5*/f3...) while((s32[]{:T(128)}, f32[320,128]{1,0:T(8,128)S(1)}, ...), condition=%wide.region_13.16_spmd, body=%wide.region_8.15_spmd.sunk | while | flops 252265920 | bytes 4767666 | solution.py:84
  127.4 12.5 %collective-permute-start = (f32[320,128]{1,0:T(8,128)S(1)}, f32[320,128]{1,0:T(8,128)S(1)}, u32[]{:S(2)}, u32[]{:S(2)}) collective-permute-start(f32[320,128]{1,0:T(8,128)S(1)} %get-tuple-element.1062), channel_id=1, source_target_pairs={{0,16},{16,32},{32,48},{48,64},{64,80},{80,96},{96,112},{112,128},... | collective-permute-start | bytes 491528 | tf_op jit(solution)/shard_map/while/body/eval_jaxpr/ppermute | solution.py:10
  142.0 4.9 collective-permute-done
  151.4 9.0 collective-permute-start
  162.5 7.9 collective-permute-done
  174.8 6.1 collective-permute-start
  183.0 10.8 collective-permute-done
  203.8 13.5 %collective-permute-done = f32[320,128]{1,0:T(8,128)S(1)} collective-permute-done((f32[320,128]{1,0:T(8,128)S(1)}, f32[320,128]{1,0:T(8,128)S(1)}, u32[]{:S(2)}, u32[]{:S(2)}) %collective-permute-start) | collective-permute-done | bytes 163872 | tf_op jit(solution)/shard_map/while/body/eval_jaxpr/ppermute | solution.py:10
  221.8 8.0 collective-permute-start
  231.8 12.4 %collective-permute-done = f32[320,128]{1,0:T(8,128)S(1)} collective-permute-done((f32[320,128]{1,0:T(8,128)S(1)}, f32[320,128]{1,0:T(8,128)S(1)}, u32[]{:S(2)}, u32[]{:S(2)}) %collective-permute-start) | collective-permute-done | bytes 163872 | tf_op jit(solution)/shard_map/while/body/eval_jaxpr/ppermute | solution.py:10
  252.7 21.9 %collective-permute-done = f32[320,128]{1,0:T(8,128)S(1)} collective-permute-done((f32[320,128]{1,0:T(8,128)S(1)}, f32[320,128]{1,0:T(8,128)S(1)}, u32[]{:S(2)}, u32[]{:S(2)}) %collective-permute-start) | collective-permute-done | bytes 163872 | tf_op jit(solution)/shard_map/while/body/eval_jaxpr/ppermute | solution.py:10
  283.1 15.7 %collective-permute-done = f32[320,128]{1,0:T(8,128)S(1)} collective-permute-done((f32[320,128]{1,0:T(8,128)S(1)}, f32[320,128]{1,0:T(8,128)S(1)}, u32[]{:S(2)}, u32[]{:S(2)}) %collective-permute-start) | collective-permute-done | bytes 163872 | tf_op jit(solution)/shard_map/while/body/eval_jaxpr/ppermute | solution.py:10
  303.2 5.7 collective-permute-start
  311.0 18.4 %collective-permute-done = f32[320,128]{1,0:T(8,128)S(1)} collective-permute-done((f32[320,128]{1,0:T(8,128)S(1)}, f32[320,128]{1,0:T(8,128)S(1)}, u32[]{:S(2)}, u32[]{:S(2)}) %collective-permute-start) | collective-permute-done | bytes 163872 | tf_op jit(solution)/shard_map/while/body/eval_jaxpr/ppermute | solution.py:10
  329.4 8.8 while.97
  342.2 19.1 %collective-permute-done = f32[320,128]{1,0:T(8,128)S(1)} collective-permute-done((f32[320,128]{1,0:T(8,128)S(1)}, f32[320,128]{1,0:T(8,128)S(1)}, u32[]{:S(2)}, u32[]{:S(2)}) %collective-permute-start) | collective-permute-done | bytes 163872 | tf_op jit(solution)/shard_map/while/body/eval_jaxpr/ppermute | solution.py:10
  372.3 21.3 %collective-permute-done = f32[320,128]{1,0:T(8,128)S(1)} collective-permute-done((f32[320,128]{1,0:T(8,128)S(1)}, f32[320,128]{1,0:T(8,128)S(1)}, u32[]{:S(2)}, u32[]{:S(2)}) %collective-permute-start) | collective-permute-done | bytes 163872 | tf_op jit(solution)/shard_map/while/body/eval_jaxpr/ppermute | solution.py:10
  402.1 22.4 %collective-permute-done = f32[320,128]{1,0:T(8,128)S(1)} collective-permute-done((f32[320,128]{1,0:T(8,128)S(1)}, f32[320,128]{1,0:T(8,128)S(1)}, u32[]{:S(2)}, u32[]{:S(2)}) %collective-permute-start) | collective-permute-done | bytes 163872 | tf_op jit(solution)/shard_map/while/body/eval_jaxpr/ppermute | solution.py:10
  433.0 22.7 %collective-permute-done = f32[320,128]{1,0:T(8,128)S(1)} collective-permute-done((f32[320,128]{1,0:T(8,128)S(1)}, f32[320,128]{1,0:T(8,128)S(1)}, u32[]{:S(2)}, u32[]{:S(2)}) %collective-permute-start) | collective-permute-done | bytes 163872 | tf_op jit(solution)/shard_map/while/body/eval_jaxpr/ppermute | solution.py:10
  455.7 7.1 collective-permute-start
  464.9 9.8 collective-permute-done
  483.1 16.4 %collective-permute-done = f32[320,128]{1,0:T(8,128)S(1)} collective-permute-done((f32[320,128]{1,0:T(8,128)S(1)}, f32[320,128]{1,0:T(8,128)S(1)}, u32[]{:S(2)}, u32[]{:S(2)}) %collective-permute-start) | collective-permute-done | bytes 163872 | tf_op jit(solution)/shard_map/while/body/eval_jaxpr/ppermute | solution.py:10
  507.9 16.7 %collective-permute-done = f32[320,128]{1,0:T(8,128)S(1)} collective-permute-done((f32[320,128]{1,0:T(8,128)S(1)}, f32[320,128]{1,0:T(8,128)S(1)}, u32[]{:S(2)}, u32[]{:S(2)}) %collective-permute-start) | collective-permute-done | bytes 163872 | tf_op jit(solution)/shard_map/while/body/eval_jaxpr/ppermute | solution.py:10
  529.8 15.1 %collective-permute-done = f32[320,128]{1,0:T(8,128)S(1)} collective-permute-done((f32[320,128]{1,0:T(8,128)S(1)}, f32[320,128]{1,0:T(8,128)S(1)}, u32[]{:S(2)}, u32[]{:S(2)}) %collective-permute-start) | collective-permute-done | bytes 163872 | tf_op jit(solution)/shard_map/while/body/eval_jaxpr/ppermute | solution.py:10
  550.3 15.6 %collective-permute-done = f32[320,128]{1,0:T(8,128)S(1)} collective-permute-done((f32[320,128]{1,0:T(8,128)S(1)}, f32[320,128]{1,0:T(8,128)S(1)}, u32[]{:S(2)}, u32[]{:S(2)}) %collective-permute-start) | collective-permute-done | bytes 163872 | tf_op jit(solution)/shard_map/while/body/eval_jaxpr/ppermute | solution.py:10
  572.1 19.4 %collective-permute-done = f32[320,128]{1,0:T(8,128)S(1)} collective-permute-done((f32[320,128]{1,0:T(8,128)S(1)}, f32[320,128]{1,0:T(8,128)S(1)}, u32[]{:S(2)}, u32[]{:S(2)}) %collective-permute-start) | collective-permute-done | bytes 163872 | tf_op jit(solution)/shard_map/while/body/eval_jaxpr/ppermute | solution.py:10
  595.5 16.6 %collective-permute-done = f32[320,128]{1,0:T(8,128)S(1)} collective-permute-done((f32[320,128]{1,0:T(8,128)S(1)}, f32[320,128]{1,0:T(8,128)S(1)}, u32[]{:S(2)}, u32[]{:S(2)}) %collective-permute-start) | collective-permute-done | bytes 163872 | tf_op jit(solution)/shard_map/while/body/eval_jaxpr/ppermute | solution.py:10
  622.1 15.3 %collective-permute-done = f32[320,128]{1,0:T(8,128)S(1)} collective-permute-done((f32[320,128]{1,0:T(8,128)S(1)}, f32[320,128]{1,0:T(8,128)S(1)}, u32[]{:S(2)}, u32[]{:S(2)}) %collective-permute-start) | collective-permute-done | bytes 163872 | tf_op jit(solution)/shard_map/while/body/eval_jaxpr/ppermute | solution.py:10
  645.8 15.7 %collective-permute-done = f32[320,128]{1,0:T(8,128)S(1)} collective-permute-done((f32[320,128]{1,0:T(8,128)S(1)}, f32[320,128]{1,0:T(8,128)S(1)}, u32[]{:S(2)}, u32[]{:S(2)}) %collective-permute-start) | collective-permute-done | bytes 163872 | tf_op jit(solution)/shard_map/while/body/eval_jaxpr/ppermute | solution.py:10
  670.0 15.0 %collective-permute-done = f32[320,128]{1,0:T(8,128)S(1)} collective-permute-done((f32[320,128]{1,0:T(8,128)S(1)}, f32[320,128]{1,0:T(8,128)S(1)}, u32[]{:S(2)}, u32[]{:S(2)}) %collective-permute-start) | collective-permute-done | bytes 163872 | tf_op jit(solution)/shard_map/while/body/eval_jaxpr/ppermute | solution.py:10
  693.5 15.1 %collective-permute-done = f32[320,128]{1,0:T(8,128)S(1)} collective-permute-done((f32[320,128]{1,0:T(8,128)S(1)}, f32[320,128]{1,0:T(8,128)S(1)}, u32[]{:S(2)}, u32[]{:S(2)}) %collective-permute-start) | collective-permute-done | bytes 163872 | tf_op jit(solution)/shard_map/while/body/eval_jaxpr/ppermute | solution.py:10
  713.0 9.8 collective-permute-start
  724.9 9.2 collective-permute-done
  738.5 7.5 collective-permute-start
  748.1 11.3 collective-permute-done
  763.8 10.4 collective-permute-start
  776.3 9.1 collective-permute-done
  789.9 27.4 %collective-permute-start = (f32[320,128]{1,0:T(8,128)S(1)}, f32[320,128]{1,0:T(8,128)S(1)}, u32[]{:S(2)}, u32[]{:S(2)}) collective-permute-start(f32[320,128]{1,0:T(8,128)S(1)} %get-tuple-element.1062), channel_id=1, source_target_pairs={{0,16},{16,32},{32,48},{48,64},{64,80},{80,96},{96,112},{112,128},... | collective-permute-start | bytes 491528 | tf_op jit(solution)/shard_map/while/body/eval_jaxpr/ppermute | solution.py:10
  819.4 4.9 collective-permute-done
  828.7 26.2 %collective-permute-start = (f32[320,128]{1,0:T(8,128)S(1)}, f32[320,128]{1,0:T(8,128)S(1)}, u32[]{:S(2)}, u32[]{:S(2)}) collective-permute-start(f32[320,128]{1,0:T(8,128)S(1)} %get-tuple-element.1062), channel_id=1, source_target_pairs={{0,16},{16,32},{32,48},{48,64},{64,80},{80,96},{96,112},{112,128},... | collective-permute-start | bytes 491528 | tf_op jit(solution)/shard_map/while/body/eval_jaxpr/ppermute | solution.py:10
  865.3 28.1 %collective-permute-start = (f32[320,128]{1,0:T(8,128)S(1)}, f32[320,128]{1,0:T(8,128)S(1)}, u32[]{:S(2)}, u32[]{:S(2)}) collective-permute-start(f32[320,128]{1,0:T(8,128)S(1)} %get-tuple-element.1062), channel_id=1, source_target_pairs={{0,16},{16,32},{32,48},{48,64},{64,80},{80,96},{96,112},{112,128},... | collective-permute-start | bytes 491528 | tf_op jit(solution)/shard_map/while/body/eval_jaxpr/ppermute | solution.py:10
  900.8 19.4 %collective-permute-start = (f32[320,128]{1,0:T(8,128)S(1)}, f32[320,128]{1,0:T(8,128)S(1)}, u32[]{:S(2)}, u32[]{:S(2)}) collective-permute-start(f32[320,128]{1,0:T(8,128)S(1)} %get-tuple-element.1062), channel_id=1, source_target_pairs={{0,16},{16,32},{32,48},{48,64},{64,80},{80,96},{96,112},{112,128},... | collective-permute-start | bytes 491528 | tf_op jit(solution)/shard_map/while/body/eval_jaxpr/ppermute | solution.py:10
  927.5 19.0 %collective-permute-start = (f32[320,128]{1,0:T(8,128)S(1)}, f32[320,128]{1,0:T(8,128)S(1)}, u32[]{:S(2)}, u32[]{:S(2)}) collective-permute-start(f32[320,128]{1,0:T(8,128)S(1)} %get-tuple-element.1062), channel_id=1, source_target_pairs={{0,16},{16,32},{32,48},{48,64},{64,80},{80,96},{96,112},{112,128},... | collective-permute-start | bytes 491528 | tf_op jit(solution)/shard_map/while/body/eval_jaxpr/ppermute | solution.py:10
  954.9 168.1 %reduce-scatter.2.cloned.1.call-done = f32[128,128]{1,0:T(8,128)} async-done(((f32[128,2048]{1,0:T(8,128)}), f32[128,128]{1,0:T(8,128)}) %reduce-scatter.2.cloned.1.call-update) | async-done | bytes 65552 | tf_op jit(solution)/shard_map/reduce_scatter | solution.py:86
  (500 shorter events, 309.2 us)
Async XLA Ops:
  6.5 107.8 %all-gather.3.cloned.1.call-start = ((), (), s32[]{:S(2)}) async-start(), calls=%async_computation.2 | async-start | bytes 2228224 | tf_op jit(solution)/shard_map/all_gather | solution.py:18
  7.3 1115.8 %reduce-scatter.2.cloned.1.call-start = ((), (), s32[]{:S(2)}) async-start(), calls=%async_computation.1 | async-start | bytes 1114112 | tf_op jit(solution)/shard_map/reduce_scatter | solution.py:86
  114.4 5.2 copy-start
  121.0 2.0 copy-start.1
  127.4 19.5 %collective-permute-start = (f32[320,128]{1,0:T(8,128)S(1)}, f32[320,128]{1,0:T(8,128)S(1)}, u32[]{:S(2)}, u32[]{:S(2)}) collective-permute-start(f32[320,128]{1,0:T(8,128)S(1)} %get-tuple-element.1062), channel_id=1, source_target_pairs={{0,16},{16,32},{32,48},{48,64},{64,80},{80,96},{96,112},{112,128},... | collective-permute-start | bytes 491528 | tf_op jit(solution)/shard_map/while/body/eval_jaxpr/ppermute | solution.py:10
  151.4 18.9 %collective-permute-start = (f32[320,128]{1,0:T(8,128)S(1)}, f32[320,128]{1,0:T(8,128)S(1)}, u32[]{:S(2)}, u32[]{:S(2)}) collective-permute-start(f32[320,128]{1,0:T(8,128)S(1)} %get-tuple-element.1062), channel_id=1, source_target_pairs={{0,16},{16,32},{32,48},{48,64},{64,80},{80,96},{96,112},{112,128},... | collective-permute-start | bytes 491528 | tf_op jit(solution)/shard_map/while/body/eval_jaxpr/ppermute | solution.py:10
  174.8 18.9 %collective-permute-start = (f32[320,128]{1,0:T(8,128)S(1)}, f32[320,128]{1,0:T(8,128)S(1)}, u32[]{:S(2)}, u32[]{:S(2)}) collective-permute-start(f32[320,128]{1,0:T(8,128)S(1)} %get-tuple-element.1062), channel_id=1, source_target_pairs={{0,16},{16,32},{32,48},{48,64},{64,80},{80,96},{96,112},{112,128},... | collective-permute-start | bytes 491528 | tf_op jit(solution)/shard_map/while/body/eval_jaxpr/ppermute | solution.py:10
  198.2 19.1 %collective-permute-start = (f32[320,128]{1,0:T(8,128)S(1)}, f32[320,128]{1,0:T(8,128)S(1)}, u32[]{:S(2)}, u32[]{:S(2)}) collective-permute-start(f32[320,128]{1,0:T(8,128)S(1)} %get-tuple-element.1062), channel_id=1, source_target_pairs={{0,16},{16,32},{32,48},{48,64},{64,80},{80,96},{96,112},{112,128},... | collective-permute-start | bytes 491528 | tf_op jit(solution)/shard_map/while/body/eval_jaxpr/ppermute | solution.py:10
  221.8 22.5 %collective-permute-start = (f32[320,128]{1,0:T(8,128)S(1)}, f32[320,128]{1,0:T(8,128)S(1)}, u32[]{:S(2)}, u32[]{:S(2)}) collective-permute-start(f32[320,128]{1,0:T(8,128)S(1)} %get-tuple-element.1062), channel_id=1, source_target_pairs={{0,16},{16,32},{32,48},{48,64},{64,80},{80,96},{96,112},{112,128},... | collective-permute-start | bytes 491528 | tf_op jit(solution)/shard_map/while/body/eval_jaxpr/ppermute | solution.py:10
  248.7 25.9 %collective-permute-start = (f32[320,128]{1,0:T(8,128)S(1)}, f32[320,128]{1,0:T(8,128)S(1)}, u32[]{:S(2)}, u32[]{:S(2)}) collective-permute-start(f32[320,128]{1,0:T(8,128)S(1)} %get-tuple-element.1062), channel_id=1, source_target_pairs={{0,16},{16,32},{32,48},{48,64},{64,80},{80,96},{96,112},{112,128},... | collective-permute-start | bytes 491528 | tf_op jit(solution)/shard_map/while/body/eval_jaxpr/ppermute | solution.py:10
  279.1 19.7 %collective-permute-start = (f32[320,128]{1,0:T(8,128)S(1)}, f32[320,128]{1,0:T(8,128)S(1)}, u32[]{:S(2)}, u32[]{:S(2)}) collective-permute-start(f32[320,128]{1,0:T(8,128)S(1)} %get-tuple-element.1062), channel_id=1, source_target_pairs={{0,16},{16,32},{32,48},{48,64},{64,80},{80,96},{96,112},{112,128},... | collective-permute-start | bytes 491528 | tf_op jit(solution)/shard_map/while/body/eval_jaxpr/ppermute | solution.py:10
  303.2 26.1 %collective-permute-start = (f32[320,128]{1,0:T(8,128)S(1)}, f32[320,128]{1,0:T(8,128)S(1)}, u32[]{:S(2)}, u32[]{:S(2)}) collective-permute-start(f32[320,128]{1,0:T(8,128)S(1)} %get-tuple-element.1062), channel_id=1, source_target_pairs={{0,16},{16,32},{32,48},{48,64},{64,80},{80,96},{96,112},{112,128},... | collective-permute-start | bytes 491528 | tf_op jit(solution)/shard_map/while/body/eval_jaxpr/ppermute | solution.py:10
  338.3 23.0 %collective-permute-start = (f32[320,128]{1,0:T(8,128)S(1)}, f32[320,128]{1,0:T(8,128)S(1)}, u32[]{:S(2)}, u32[]{:S(2)}) collective-permute-start(f32[320,128]{1,0:T(8,128)S(1)} %get-tuple-element.1062), channel_id=1, source_target_pairs={{0,16},{16,32},{32,48},{48,64},{64,80},{80,96},{96,112},{112,128},... | collective-permute-start | bytes 491528 | tf_op jit(solution)/shard_map/while/body/eval_jaxpr/ppermute | solution.py:10
  365.8 27.9 %collective-permute-start = (f32[320,128]{1,0:T(8,128)S(1)}, f32[320,128]{1,0:T(8,128)S(1)}, u32[]{:S(2)}, u32[]{:S(2)}) collective-permute-start(f32[320,128]{1,0:T(8,128)S(1)} %get-tuple-element.1062), channel_id=1, source_target_pairs={{0,16},{16,32},{32,48},{48,64},{64,80},{80,96},{96,112},{112,128},... | collective-permute-start | bytes 491528 | tf_op jit(solution)/shard_map/while/body/eval_jaxpr/ppermute | solution.py:10
  398.1 26.4 %collective-permute-start = (f32[320,128]{1,0:T(8,128)S(1)}, f32[320,128]{1,0:T(8,128)S(1)}, u32[]{:S(2)}, u32[]{:S(2)}) collective-permute-start(f32[320,128]{1,0:T(8,128)S(1)} %get-tuple-element.1062), channel_id=1, source_target_pairs={{0,16},{16,32},{32,48},{48,64},{64,80},{80,96},{96,112},{112,128},... | collective-permute-start | bytes 491528 | tf_op jit(solution)/shard_map/while/body/eval_jaxpr/ppermute | solution.py:10
  429.0 26.7 %collective-permute-start = (f32[320,128]{1,0:T(8,128)S(1)}, f32[320,128]{1,0:T(8,128)S(1)}, u32[]{:S(2)}, u32[]{:S(2)}) collective-permute-start(f32[320,128]{1,0:T(8,128)S(1)} %get-tuple-element.1062), channel_id=1, source_target_pairs={{0,16},{16,32},{32,48},{48,64},{64,80},{80,96},{96,112},{112,128},... | collective-permute-start | bytes 491528 | tf_op jit(solution)/shard_map/while/body/eval_jaxpr/ppermute | solution.py:10
  455.7 18.9 %collective-permute-start = (f32[320,128]{1,0:T(8,128)S(1)}, f32[320,128]{1,0:T(8,128)S(1)}, u32[]{:S(2)}, u32[]{:S(2)}) collective-permute-start(f32[320,128]{1,0:T(8,128)S(1)} %get-tuple-element.1062), channel_id=1, source_target_pairs={{0,16},{16,32},{32,48},{48,64},{64,80},{80,96},{96,112},{112,128},... | collective-permute-start | bytes 491528 | tf_op jit(solution)/shard_map/while/body/eval_jaxpr/ppermute | solution.py:10
  479.2 20.3 %collective-permute-start = (f32[320,128]{1,0:T(8,128)S(1)}, f32[320,128]{1,0:T(8,128)S(1)}, u32[]{:S(2)}, u32[]{:S(2)}) collective-permute-start(f32[320,128]{1,0:T(8,128)S(1)} %get-tuple-element.1062), channel_id=1, source_target_pairs={{0,16},{16,32},{32,48},{48,64},{64,80},{80,96},{96,112},{112,128},... | collective-permute-start | bytes 491528 | tf_op jit(solution)/shard_map/while/body/eval_jaxpr/ppermute | solution.py:10
  504.0 20.7 %collective-permute-start = (f32[320,128]{1,0:T(8,128)S(1)}, f32[320,128]{1,0:T(8,128)S(1)}, u32[]{:S(2)}, u32[]{:S(2)}) collective-permute-start(f32[320,128]{1,0:T(8,128)S(1)} %get-tuple-element.1062), channel_id=1, source_target_pairs={{0,16},{16,32},{32,48},{48,64},{64,80},{80,96},{96,112},{112,128},... | collective-permute-start | bytes 491528 | tf_op jit(solution)/shard_map/while/body/eval_jaxpr/ppermute | solution.py:10
  524.8 20.1 %collective-permute-start = (f32[320,128]{1,0:T(8,128)S(1)}, f32[320,128]{1,0:T(8,128)S(1)}, u32[]{:S(2)}, u32[]{:S(2)}) collective-permute-start(f32[320,128]{1,0:T(8,128)S(1)} %get-tuple-element.1062), channel_id=1, source_target_pairs={{0,16},{16,32},{32,48},{48,64},{64,80},{80,96},{96,112},{112,128},... | collective-permute-start | bytes 491528 | tf_op jit(solution)/shard_map/while/body/eval_jaxpr/ppermute | solution.py:10
  545.0 20.8 %collective-permute-start = (f32[320,128]{1,0:T(8,128)S(1)}, f32[320,128]{1,0:T(8,128)S(1)}, u32[]{:S(2)}, u32[]{:S(2)}) collective-permute-start(f32[320,128]{1,0:T(8,128)S(1)} %get-tuple-element.1062), channel_id=1, source_target_pairs={{0,16},{16,32},{32,48},{48,64},{64,80},{80,96},{96,112},{112,128},... | collective-permute-start | bytes 491528 | tf_op jit(solution)/shard_map/while/body/eval_jaxpr/ppermute | solution.py:10
  565.9 25.5 %collective-permute-start = (f32[320,128]{1,0:T(8,128)S(1)}, f32[320,128]{1,0:T(8,128)S(1)}, u32[]{:S(2)}, u32[]{:S(2)}) collective-permute-start(f32[320,128]{1,0:T(8,128)S(1)} %get-tuple-element.1062), channel_id=1, source_target_pairs={{0,16},{16,32},{32,48},{48,64},{64,80},{80,96},{96,112},{112,128},... | collective-permute-start | bytes 491528 | tf_op jit(solution)/shard_map/while/body/eval_jaxpr/ppermute | solution.py:10
  591.5 20.6 %collective-permute-start = (f32[320,128]{1,0:T(8,128)S(1)}, f32[320,128]{1,0:T(8,128)S(1)}, u32[]{:S(2)}, u32[]{:S(2)}) collective-permute-start(f32[320,128]{1,0:T(8,128)S(1)} %get-tuple-element.1062), channel_id=1, source_target_pairs={{0,16},{16,32},{32,48},{48,64},{64,80},{80,96},{96,112},{112,128},... | collective-permute-start | bytes 491528 | tf_op jit(solution)/shard_map/while/body/eval_jaxpr/ppermute | solution.py:10
  616.6 20.8 %collective-permute-start = (f32[320,128]{1,0:T(8,128)S(1)}, f32[320,128]{1,0:T(8,128)S(1)}, u32[]{:S(2)}, u32[]{:S(2)}) collective-permute-start(f32[320,128]{1,0:T(8,128)S(1)} %get-tuple-element.1062), channel_id=1, source_target_pairs={{0,16},{16,32},{32,48},{48,64},{64,80},{80,96},{96,112},{112,128},... | collective-permute-start | bytes 491528 | tf_op jit(solution)/shard_map/while/body/eval_jaxpr/ppermute | solution.py:10
  641.9 19.7 %collective-permute-start = (f32[320,128]{1,0:T(8,128)S(1)}, f32[320,128]{1,0:T(8,128)S(1)}, u32[]{:S(2)}, u32[]{:S(2)}) collective-permute-start(f32[320,128]{1,0:T(8,128)S(1)} %get-tuple-element.1062), channel_id=1, source_target_pairs={{0,16},{16,32},{32,48},{48,64},{64,80},{80,96},{96,112},{112,128},... | collective-permute-start | bytes 491528 | tf_op jit(solution)/shard_map/while/body/eval_jaxpr/ppermute | solution.py:10
  666.0 19.0 %collective-permute-start = (f32[320,128]{1,0:T(8,128)S(1)}, f32[320,128]{1,0:T(8,128)S(1)}, u32[]{:S(2)}, u32[]{:S(2)}) collective-permute-start(f32[320,128]{1,0:T(8,128)S(1)} %get-tuple-element.1062), channel_id=1, source_target_pairs={{0,16},{16,32},{32,48},{48,64},{64,80},{80,96},{96,112},{112,128},... | collective-permute-start | bytes 491528 | tf_op jit(solution)/shard_map/while/body/eval_jaxpr/ppermute | solution.py:10
  689.5 19.0 %collective-permute-start = (f32[320,128]{1,0:T(8,128)S(1)}, f32[320,128]{1,0:T(8,128)S(1)}, u32[]{:S(2)}, u32[]{:S(2)}) collective-permute-start(f32[320,128]{1,0:T(8,128)S(1)} %get-tuple-element.1062), channel_id=1, source_target_pairs={{0,16},{16,32},{32,48},{48,64},{64,80},{80,96},{96,112},{112,128},... | collective-permute-start | bytes 491528 | tf_op jit(solution)/shard_map/while/body/eval_jaxpr/ppermute | solution.py:10
  713.0 21.0 %collective-permute-start = (f32[320,128]{1,0:T(8,128)S(1)}, f32[320,128]{1,0:T(8,128)S(1)}, u32[]{:S(2)}, u32[]{:S(2)}) collective-permute-start(f32[320,128]{1,0:T(8,128)S(1)} %get-tuple-element.1062), channel_id=1, source_target_pairs={{0,16},{16,32},{32,48},{48,64},{64,80},{80,96},{96,112},{112,128},... | collective-permute-start | bytes 491528 | tf_op jit(solution)/shard_map/while/body/eval_jaxpr/ppermute | solution.py:10
  738.5 20.9 %collective-permute-start = (f32[320,128]{1,0:T(8,128)S(1)}, f32[320,128]{1,0:T(8,128)S(1)}, u32[]{:S(2)}, u32[]{:S(2)}) collective-permute-start(f32[320,128]{1,0:T(8,128)S(1)} %get-tuple-element.1062), channel_id=1, source_target_pairs={{0,16},{16,32},{32,48},{48,64},{64,80},{80,96},{96,112},{112,128},... | collective-permute-start | bytes 491528 | tf_op jit(solution)/shard_map/while/body/eval_jaxpr/ppermute | solution.py:10
  763.8 21.6 %collective-permute-start = (f32[320,128]{1,0:T(8,128)S(1)}, f32[320,128]{1,0:T(8,128)S(1)}, u32[]{:S(2)}, u32[]{:S(2)}) collective-permute-start(f32[320,128]{1,0:T(8,128)S(1)} %get-tuple-element.1062), channel_id=1, source_target_pairs={{0,16},{16,32},{32,48},{48,64},{64,80},{80,96},{96,112},{112,128},... | collective-permute-start | bytes 491528 | tf_op jit(solution)/shard_map/while/body/eval_jaxpr/ppermute | solution.py:10
  789.9 34.3 %collective-permute-start = (f32[320,128]{1,0:T(8,128)S(1)}, f32[320,128]{1,0:T(8,128)S(1)}, u32[]{:S(2)}, u32[]{:S(2)}) collective-permute-start(f32[320,128]{1,0:T(8,128)S(1)} %get-tuple-element.1062), channel_id=1, source_target_pairs={{0,16},{16,32},{32,48},{48,64},{64,80},{80,96},{96,112},{112,128},... | collective-permute-start | bytes 491528 | tf_op jit(solution)/shard_map/while/body/eval_jaxpr/ppermute | solution.py:10
  828.7 32.1 %collective-permute-start = (f32[320,128]{1,0:T(8,128)S(1)}, f32[320,128]{1,0:T(8,128)S(1)}, u32[]{:S(2)}, u32[]{:S(2)}) collective-permute-start(f32[320,128]{1,0:T(8,128)S(1)} %get-tuple-element.1062), channel_id=1, source_target_pairs={{0,16},{16,32},{32,48},{48,64},{64,80},{80,96},{96,112},{112,128},... | collective-permute-start | bytes 491528 | tf_op jit(solution)/shard_map/while/body/eval_jaxpr/ppermute | solution.py:10
  865.3 30.9 %collective-permute-start = (f32[320,128]{1,0:T(8,128)S(1)}, f32[320,128]{1,0:T(8,128)S(1)}, u32[]{:S(2)}, u32[]{:S(2)}) collective-permute-start(f32[320,128]{1,0:T(8,128)S(1)} %get-tuple-element.1062), channel_id=1, source_target_pairs={{0,16},{16,32},{32,48},{48,64},{64,80},{80,96},{96,112},{112,128},... | collective-permute-start | bytes 491528 | tf_op jit(solution)/shard_map/while/body/eval_jaxpr/ppermute | solution.py:10
  900.8 22.3 %collective-permute-start = (f32[320,128]{1,0:T(8,128)S(1)}, f32[320,128]{1,0:T(8,128)S(1)}, u32[]{:S(2)}, u32[]{:S(2)}) collective-permute-start(f32[320,128]{1,0:T(8,128)S(1)} %get-tuple-element.1062), channel_id=1, source_target_pairs={{0,16},{16,32},{32,48},{48,64},{64,80},{80,96},{96,112},{112,128},... | collective-permute-start | bytes 491528 | tf_op jit(solution)/shard_map/while/body/eval_jaxpr/ppermute | solution.py:10
  927.5 21.8 %collective-permute-start = (f32[320,128]{1,0:T(8,128)S(1)}, f32[320,128]{1,0:T(8,128)S(1)}, u32[]{:S(2)}, u32[]{:S(2)}) collective-permute-start(f32[320,128]{1,0:T(8,128)S(1)} %get-tuple-element.1062), channel_id=1, source_target_pairs={{0,16},{16,32},{32,48},{48,64},{64,80},{80,96},{96,112},{112,128},... | collective-permute-start | bytes 491528 | tf_op jit(solution)/shard_map/while/body/eval_jaxpr/ppermute | solution.py:10
Sparse Core Ops, SparseCore 0:
  9.4 104.8 all-gather.2
  955.0 167.9 reduce-scatter.1
where the time goes:
time: 1130 us
  waiting for transfers between devices  649 us (57%)
  starting transfers between devices  239 us (21%)
  local copies, waits for them, and re-layouts  85.6 us (8%)
  loops' own time  65.1 us (6%)
  matrix products  40.9 us (4%)
  other arithmetic  35.6 us (3%)
  between operations  14.7 us (1%)
    ppermute x31, waiting for transfers between devices, from_behind(): return lax.ppermute(value, axis, pairs)  402 us
    ppermute x31, starting transfers between devices, from_behind(): return lax.ppermute(value, axis, pairs)  239 us
    reduce_scatter x1, waiting for transfers between devices, shards(): lax.psum_scatter(partial_value, 'rep', scatter_dimension=1, tiled=True)  168 us
    all_gather x1, waiting for transfers between devices, shards(): gathered = lax.all_gather(coords, 'rep', axis=0, tiled=True)  77.7 us
    another operation x1, loops' own time, shards(): totals = lax.fori_loop(1, cycle_size, onward_turn, (panel, totals))[1]  43.7 us
    dot_general x28, matrix products, one_group(): jnp.einsum('fgt,fu->gtu', row_block, col_coords, precision=lax.Precision....  30.2 us
  transfers between devices with their start and end apart: 33, of which 33 were waited for; matrix products, arithmetic and copies ran while one was open for 4% of the time, Pallas kernels for 0%

commit v1 on v0

v1 whole, which is shorter than its diff:
```python
import functools
import math

import jax
import jax.numpy as jnp
from jax import lax
from jax.experimental import pallas as pl
from jax.experimental.pallas import tpu as pltpu
from jax.sharding import PartitionSpec as P

MESH = pl.DeviceIdType.MESH
X, Y, Z = 4, 4, 16
HALF = Z // 2
PLANE = X * Y
FEAT, EIG, BLOCK = 192, 128, 128
PANEL = FEAT + EIG
PART = 12
PART_PAD = 16
REP = 16
ROOT = math.sqrt(2.0 * math.log2(math.e) / FEAT)


def rem(a, b):
    return lax.rem(a, jnp.int32(b))


def place():
    blk, rep = lax.axis_index("blk"), lax.axis_index("rep")
    core, zl = rem(rep, 2), rep // 2
    zh, xy = rem(blk, 2), blk // 2
    return blk, rep, core, xy // Y, rem(xy, Y), zh * HALF + zl


def device(x, y, z, core):
    return {"blk": (x * Y + y) * 2 + z // HALF, "rep": rem(z, HALF) * 2 + core}


def copy_to(src, dst, send, recv, where):
    return pltpu.make_async_remote_copy(
        src_ref=src, dst_ref=dst, send_sem=send, recv_sem=recv, device_id=where, device_id_type=MESH
    )


def scale_of(x):
    return jnp.exp2(-0.5 * jnp.sum(x * x, axis=0, keepdims=True))


def gather_kernel(
    parts, vecs, lists, rows, cols, far_lists, own_scale, landed,
    part_send, part_recv, list_send, list_recv, z_send, z_recv, xy_send, xy_recv, pair_send, pair_recv,
):
    blk, rep, core, x, y, z = place()
    other = 1 - core
    here = device(x, y, z, core)
    up, down = rem(z + 1, Z), rem(z + Z - 1, Z)
    far = rem(z + HALF, Z)

    barrier = pltpu.get_barrier_semaphore()
    mates = [{"blk": blk, "rep": rem(rep + d, REP)} for d in range(1, REP)]
    mates += [device(x, y, up, core), device(x, y, down, core), device(x, y, far, core)]
    mates += [device(rem(x + d, X), y, z, core) for d in (1, X - 1)]
    mates += [device(x, rem(y + d, Y), z, core) for d in (1, Y - 1)]
    for mate in mates:
        pl.semaphore_signal(barrier, inc=1, device_id=mate, device_id_type=MESH)
    pl.semaphore_wait(barrier, len(mates))

    for d in range(1, REP):
        to = rem(rep + d, REP)
        copy_to(parts.at[to], landed.at[rep], part_send, part_recv, {"blk": blk, "rep": to}).start()
    cols[x * Y + y, core, FEAT:] = vecs[...]
    landed[rep] = parts[rep]
    copy_to(lists, far_lists, list_send, list_recv, device(x, y, far, core)).start()

    def plane_steps(phase, base, size):
        half, quarter = size // 2, size // 4

        def spot(turn, i, j):
            dx, dy = (i, j) if turn == 0 else (j, i)
            return rem(x + dx + X, X), rem(y + dy + Y, Y)

        def region(turn, i, j, part):
            sx, sy = spot(turn, i, j)
            start, count = base + turn * half, half
            if part is not None:
                start, count = start + part * quarter, quarter
            return cols.at[sx * Y + sy, core, pl.ds(start, count)]

        def send(turn, slot, i, j, part, to):
            tx, ty = spot(turn, *to)
            ref = region(turn, i, j, part)
            src = vecs.at[pl.ds(turn * half, half)] if phase == 0 and (i, j) == (0, 0) else ref
            copy_to(src, ref, xy_send, xy_recv.at[phase, turn * 20 + slot], device(tx, ty, z, core)).start()

        def arrive(turn, slot, i, j, part):
            ref = region(turn, i, j, part)
            copy_to(ref, ref, xy_send, xy_recv.at[phase, turn * 20 + slot], here).wait_recv()

        def share(turn, i, j):
            ref = region(turn, i, j, None)
            src = vecs.at[pl.ds(turn * half, half)] if phase == 0 and (i, j) == (0, 0) else ref
            copy_to(src, ref, pair_send, pair_recv, device(x, y, z, other)).start()

        def spread(n, i):
            for turn in range(2):
                send(turn, 4 + 4 * n, i, 0, None, (0, 1))
                send(turn, 5 + 4 * n, i, 0, None, (0, -1))

        def relay(n, i):
            for turn in range(2):
                arrive(turn, 4 + 4 * n, i, -1, None)
                send(turn, 6 + 4 * n, i, -1, 0, (0, 1))
                share(turn, i, -1)
                arrive(turn, 5 + 4 * n, i, 1, None)
                send(turn, 7 + 4 * n, i, 1, 1, (0, -1))
                share(turn, i, 1)

        def finish(n, i):
            for turn in range(2):
                arrive(turn, 6 + 4 * n, i, 2, 0)
                arrive(turn, 7 + 4 * n, i, 2, 1)
                share(turn, i, 2)

        for turn in range(2):
            send(turn, 0, 0, 0, None, (1, 0))
            send(turn, 1, 0, 0, None, (-1, 0))
        spread(0, 0)
        for turn in range(2):
            share(turn, 0, 0)
        yield
        for turn in range(2):
            arrive(turn, 0, -1, 0, None)
            send(turn, 2, -1, 0, 0, (1, 0))
            arrive(turn, 1, 1, 0, None)
            send(turn, 3, 1, 0, 1, (-1, 0))
        spread(1, -1)
        spread(2, 1)
        for turn in range(2):
            share(turn, -1, 0)
            share(turn, 1, 0)
        yield
        relay(0, 0)
        for turn in range(2):
            arrive(turn, 2, 2, 0, 0)
            arrive(turn, 3, 2, 0, 1)
        spread(3, 2)
        for turn in range(2):
            share(turn, 2, 0)
        yield
        relay(1, -1)
        relay(2, 1)
        yield
        relay(3, 2)
        finish(0, 0)
        yield
        finish(1, -1)
        finish(2, 1)
        finish(3, 2)

    def ring_steps():
        size = FEAT // 2

        def region(t, part):
            return rows.at[rem(z + t + Z, Z), pl.ds(part * size, size)]

        def send(t, way, part):
            ref = region(-t * way, part)
            sem = z_recv.at[(0 if way > 0 else 16) + 2 * t + part]
            copy_to(ref, ref, z_send, sem, device(x, y, up if way > 0 else down, core)).start()

        def arrive(t, way, part):
            ref = region(-t * way, part)
            sem = z_recv.at[(0 if way > 0 else 16) + 2 * (t - 1) + part]
            copy_to(ref, ref, z_send, sem, here).wait_recv()

        for part in range(2):
            send(0, 1, part)
            send(0, -1, part)
        yield
        for t in range(1, HALF):
            for part in range(2):
                for way in (1, -1):
                    arrive(t, way, part)
                    if t < HALF - 1 or part == (0 if way > 0 else 1):
                        send(t, way, part)
            yield
        arrive(HALF, 1, 0)
        arrive(HALF, -1, 1)

    for _ in plane_steps(0, FEAT, EIG):
        pass
    gone = copy_to(parts.at[pl.ds(0, REP - 1)], landed.at[pl.ds(0, REP - 1)], part_send, part_recv, here)
    gone.wait_recv()
    me = x * Y + y
    for p in range(REP):
        piece = landed[p, :PART, :] * ROOT
        rows[z, p * PART : (p + 1) * PART] = piece
        cols[me, core, p * PART : (p + 1) * PART] = piece
    ring, plane = ring_steps(), plane_steps(1, 0, FEAT)
    going = True
    while going:
        going = next(ring, "end") != "end"
        going = next(plane, "end") != "end" or going
    own_scale[...] = jnp.broadcast_to(scale_of(rows[z]), own_scale.shape)

    gone.wait_send()
    copy_to(lists, far_lists, list_send, list_recv, here).wait()
    fill = rows.at[pl.ds(0, Z - 1)]
    copy_to(fill, fill, z_send, z_recv.at[0], here).wait_send()
    fill = cols.at[pl.ds(0, PLANE - 1), core]
    copy_to(fill, fill, xy_send, xy_recv.at[0, 0], here).wait_send()
    fill = cols.at[:, core]
    copy_to(fill, fill, pair_send, pair_recv, here).wait_send()
    fill = cols.at[:, other]
    copy_to(fill, fill, pair_send, pair_recv, here).wait_recv()


def halves(value):
    high = value.astype(jnp.bfloat16)
    low = (value - high.astype(jnp.float32)).astype(jnp.bfloat16)
    return high, low


def compute_kernel(listed, rows, cols, out, row_ops, col_ops, vec_ops, picks):
    n_rows, n_cols = rows.shape[0], cols.shape[0]

    @pl.loop(0, n_rows)
    def _(r):
        high, low = halves(rows[r])
        both = jnp.concatenate([high.astype(jnp.float32), low.astype(jnp.float32)], axis=0)
        flipped = both.T.astype(jnp.bfloat16)
        row_ops[r, :, : 2 * FEAT] = flipped
        row_ops[r, :, 2 * FEAT :] = flipped

    @pl.loop(0, n_cols)
    def _(q):
        coords = cols[q, :FEAT]
        high, low = halves(coords)
        col_ops[q, :FEAT] = high
        col_ops[q, FEAT : 2 * FEAT] = high
        col_ops[q, 2 * FEAT : 3 * FEAT] = low
        col_ops[q, 3 * FEAT :] = low
        vecs = cols[q, FEAT:] * scale_of(coords)
        high, low = halves(vecs.T)
        vec_ops[q, 0] = high
        vec_ops[q, 1] = low

    vec_ops[n_cols] = jnp.zeros_like(vec_ops[n_cols])
    col_ops[n_cols] = jnp.zeros_like(col_ops[n_cols])

    @pl.loop(0, n_rows)
    def _(r):
        count = jnp.int32(0)
        for q in range(n_cols):
            picks[count] = q
            count = count + listed[r, q]
        picks[count] = n_cols
        out[r] = jnp.zeros_like(out[r])

        @pl.loop(0, (count + 1) // 2)
        def _(step):
            a, b = picks[2 * step], picks[2 * step + 1]
            col = jnp.concatenate([col_ops[a], col_ops[b]], axis=1)
            power = jnp.dot(row_ops[r], col, preferred_element_type=jnp.float32)
            high, low = halves(jnp.exp2(power))
            vec_high = jnp.concatenate([vec_ops[a, 0], vec_ops[b, 0]], axis=0)
            vec_low = jnp.concatenate([vec_ops[a, 1], vec_ops[b, 1]], axis=0)
            out[r] += (
                jnp.dot(high, vec_high, preferred_element_type=jnp.float32)
                + jnp.dot(high, vec_low, preferred_element_type=jnp.float32)
                + jnp.dot(low, vec_high, preferred_element_type=jnp.float32)
            )


def reduce_kernel(partial, own_scale, out, up_in, down_in, up_sum, down_sum, up_send, up_recv, down_send, down_recv):
    _, _, core, x, y, z = place()
    here = device(x, y, z, core)
    up, down = device(x, y, rem(z + 1, Z), core), device(x, y, rem(z + Z - 1, Z), core)
    barrier = pltpu.get_barrier_semaphore()
    for mate in (up, down):
        pl.semaphore_signal(barrier, inc=1, device_id=mate, device_id_type=MESH)
    pl.semaphore_wait(barrier, 2)
    size = BLOCK // 2
    ways = (
        (1, up, up_in, up_sum, up_send, up_recv),
        (-1, down, down_in, down_sum, down_send, down_recv),
    )

    def slot(step, part):
        return 2 * step - part

    for step in range(HALF):
        for lead in range(2):
            for way, to, landing, sums, send, recv in ways:
                if step == 0 and lead == 1:
                    continue
                part = lead if way > 0 else 1 - lead
                mine = partial.at[rem(z + way * (HALF - step) + Z, Z), pl.ds(part * size, size)]
                first = step == 0 if lead == 0 else step == 1
                at = slot(step, lead)
                if first:
                    src = mine
                else:
                    before = slot(step - 1, lead)
                    ref = landing.at[before]
                    copy_to(ref, ref, send, recv.at[before], here).wait_recv()
                    sums[at] = mine[...] + landing[before]
                    src = sums.at[at]
                copy_to(src, landing.at[at], send, recv.at[at], to).start()
    for part in range(2):
        total = partial[z, part * size : (part + 1) * size]
        for way, to, landing, sums, send, recv in ways:
            lead = part if way > 0 else 1 - part
            at = slot(HALF - 1, lead)
            ref = landing.at[at]
            copy_to(ref, ref, send, recv.at[at], here).wait_recv()
            total = total + landing[at]
        out[:, part * size : (part + 1) * size] = total.T * own_scale[:1, part * size : (part + 1) * size]
    for way, to, landing, sums, send, recv in ways:
        copy_to(landing, landing, send, recv.at[0], here).wait_send()


def shards(coords, eigvecs, nbr_list, nbr_count):
    f32 = jnp.float32
    vmem = pl.BlockSpec(memory_space=pltpu.VMEM)
    dma = pltpu.SemaphoreType.DMA
    _, rep, core, _, _, z = place()
    zh, zl = z // HALF, rem(z, HALF)

    parts = coords.reshape(PART, REP, BLOCK).transpose(1, 0, 2)
    parts = jnp.pad(parts, ((0, 0), (0, PART_PAD - PART), (0, 0)))
    slots = lax.broadcasted_iota(jnp.int32, nbr_list.shape, 1)
    lists = jnp.where(slots < nbr_count[:, None], nbr_list, -1)

    rows, cols, far_lists, own_scale = pl.pallas_call(
        gather_kernel,
        out_shape=(
            jax.ShapeDtypeStruct((Z, FEAT, BLOCK), f32),
            jax.ShapeDtypeStruct((PLANE, 2, PANEL, BLOCK), f32),
            jax.ShapeDtypeStruct(lists.shape, jnp.int32),
            jax.ShapeDtypeStruct((8, BLOCK), f32),
        ),
        in_specs=[vmem] * 3,
        out_specs=(vmem,) * 4,
        scratch_shapes=[
            pltpu.VMEM((REP, PART_PAD, BLOCK), f32),
            dma, dma, dma, dma, dma, dma((32,)), dma, dma((2, 40)), dma, dma,
        ],
        compiler_params=pltpu.CompilerParams(collective_id=0, has_side_effects=True),
    )(parts, eigvecs, lists)

    both = jnp.stack([lists, far_lists]).reshape(2, HALF, 2, BLOCK)
    both = jnp.where(core == 0, both[:, :, 0], both[:, :, 1])
    wanted = jnp.where(zh == 0, both, both[::-1]).reshape(Z, BLOCK)
    q = jnp.arange(2 * PLANE, dtype=jnp.int32)
    names = ((q // 2) * 2 + zh) * REP + zl * 2 + q % 2
    listed = jnp.any(wanted[:, None, :] == names[None, :, None], axis=-1).astype(jnp.int32)

    n_cols = 2 * PLANE
    partial = pl.pallas_call(
        compute_kernel,
        out_shape=jax.ShapeDtypeStruct((Z, BLOCK, EIG), f32),
        in_specs=[pl.BlockSpec(memory_space=pltpu.SMEM), vmem, vmem],
        out_specs=vmem,
        scratch_shapes=[
            pltpu.VMEM((Z, BLOCK, 4 * FEAT), jnp.bfloat16),
            pltpu.VMEM((n_cols + 1, 4 * FEAT, BLOCK), jnp.bfloat16),
            pltpu.VMEM((n_cols + 1, 2, BLOCK, EIG), jnp.bfloat16),
            pltpu.SMEM((n_cols + 8,), jnp.int32),
        ],
    )(listed, rows, cols.reshape(n_cols, PANEL, BLOCK))

    size = BLOCK // 2
    return pl.pallas_call(
        reduce_kernel,
        out_shape=jax.ShapeDtypeStruct((EIG, BLOCK), f32),
        in_specs=[vmem] * 2,
        out_specs=vmem,
        scratch_shapes=[pltpu.VMEM((2 * HALF - 1, size, EIG), f32)] * 4
        + [dma, dma((2 * HALF - 1,)), dma, dma((2 * HALF - 1,))],
        compiler_params=pltpu.CompilerParams(collective_id=1, has_side_effects=True),
    )(partial, own_scale)


def solution(mesh):
    return jax.shard_map(
        shards,
        mesh=mesh,
        in_specs=(P("rep", "blk"), P(None, ("blk", "rep")), P("blk", None), P("blk")),
        out_specs=P(None, ("blk", "rep")),
        check_vma=False,
    )
```

time: 1130 us -> 133 us (0.12)
  waiting for transfers between devices: 649 us -> 0 us
  starting transfers between devices: 239 us -> 0 us
  Pallas kernels: 0 us -> 124 us
  local copies, waits for them, and re-layouts: 85.6 us -> 3.1 us
  loops' own time: 65.1 us -> 0 us
  matrix products: 40.9 us -> 0 us
  other arithmetic: 35.6 us -> 3.21 us
  between operations: 14.7 us -> 0.05 us
    ppermute x31 -> x0, waiting for transfers between devices: 402 us -> none  [from_behind(): return lax.ppermute(value, axis, pairs)]
    ppermute x31 -> x0, starting transfers between devices: 239 us -> none  [from_behind(): return lax.ppermute(value, axis, pairs)]
    reduce_scatter x1 -> x0, waiting for transfers between devices: 168 us -> none  [shards(): lax.psum_scatter(partial_value, 'rep', scatter_dimension=1, tiled=True)]
    pallas_call x0 -> x3, Pallas kernels: none -> 124 us  [the longest x1 62.3 us: shards(): pl.pallas_call(gather_kernel, out_shape=(jax.ShapeDtypeStruct((Z, FEAT, B...]
    all_gather x1 -> x0, waiting for transfers between devices: 77.7 us -> none  [shards(): gathered = lax.all_gather(coords, 'rep', axis=0, tiled=True)]
    another operation x34 -> x0, loops' own time: 65.1 us -> none  [the longest x1 43.7 us: shards(): totals = lax.fori_loop(1, cycle_size, onward_turn, (panel, totals))[1]]
    gather x69 -> x0, local copies, waits for them, and re-layouts: 52.8 us -> none  [the longest x28 16 us: one_group(): row_block = jnp.take(row_tiles, picked, axis=1)]
    dot_general x56 -> x0, matrix products: 40.9 us -> none  [the longest x28 30.2 us: one_group(): jnp.einsum('fgt,fu->gtu', row_block, col_coords, precision=lax.Precision....]
  transfers between devices with their start and end apart: 33 -> 0, of which waited for: 33 -> 0; matrix products, arithmetic and copies ran while one was open for 4% -> 0% of each run, Pallas kernels for 0% -> 0%
where the time goes in v1:
time: 133 us; the launch traced here: 130 us
  Pallas kernels  124 us (93%)
  other arithmetic  3.21 us (2%)
  local copies, waits for them, and re-layouts  3.1 us (2%)
    pallas_call x1, Pallas kernels, shards(): pl.pallas_call(gather_kernel, out_shape=(jax.ShapeDtypeStruct((Z, FEAT, B...  62.3 us
    pallas_call x1, Pallas kernels, shards(): pl.pallas_call(reduce_kernel, out_shape=jax.ShapeDtypeStruct((EIG, BLOCK)...  36.2 us
    pallas_call x1, Pallas kernels, shards(): pl.pallas_call(compute_kernel, out_shape=jax.ShapeDtypeStruct((Z, BLOCK,...  25.6 us

profile of v1, /device:TPU:6, one launch (start us, length us, event | category | flops | bytes accessed | tf_op | source)
XLA Modules:
  0.0 130.5 jit_solution(16198651674390984864)
XLA Ops:
  0.0 1.4 %fusion.2.lists = s32[16,128]{1,0:T(8,128)} fusion(s32[16,128]{1,0:T(8,128)} %param.6, s32[16]{0:T(128)} %param.7), kind=kLoop, calls=%fused_computation.10 | loop fusion | flops 4096 | bytes 16448 | tf_op jit(solution)/shard_map/jit(_where)/select_n | solution.py:332
  1.4 0.9 copy.7
  2.4 0.7 pad.4.parts
  3.0 62.3 %shard_map.46 = (f32[16,192,128]{2,1,0:T(8,128)}, f32[16,2,320,128]{3,2,1,0:T(8,128)}, s32[16,128]{1,0:T(8,128)}, f32[8,128]{1,0:T(8,128)}) custom-call(f32[16,16,128]{2,1,0:T(8,128)} %pad.4.parts, f32[128,128]{1,0:T(8,128)} %vecs.1, s32[16,128]{1,0:T(8,128)} %fusion.2.lists), custom_call_target="tpu_custom_call" | custom-call | tf_op jit(solution)/shard_map/pallas_call | solution.py:334
  65.4 0.8 broadcast_select_fusion
  66.2 0.4 compare_reduce_fusion
  66.6 0.6 convert_element_type.5.listed
  67.2 25.6 %shard_map.47.partial = f32[16,128,128]{2,1,0:T(8,128)} custom-call(s32[16,32]{1,0:T(8,128)} %convert_element_type.5.listed, f32[16,192,128]{2,1,0:T(8,128)} %get-tuple-element.10.rows, f32[32,320,128]{2,1,0:T(8,128)} %bitcast.12), custom_call_target="tpu_custom_call" | custom-call | tf_op jit(solution)/shard_map/pallas_call | solution.py:359
  92.8 36.2 %shard_map.48 = f32[128,128]{1,0:T(8,128)} custom-call(f32[16,128,128]{2,1,0:T(8,128)} %shard_map.47.partial, f32[8,128]{1,0:T(8,128)} %get-tuple-element.12.own_scale), custom_call_target="tpu_custom_call" | custom-call | tf_op jit(solution)/shard_map/pallas_call | solution.py:373
  129.0 1.5 %copy.11 = f32[128,128]{1,0:T(8,128)} copy(f32[128,128]{1,0:T(8,128)} %shard_map.48) | data formatting | bytes 131072
  (4 shorter events, 0.1 us)

commit v2 on v1

v2 whole, which is shorter than its diff:
```python
import math

import jax
import jax.numpy as jnp
from jax import lax
from jax.experimental import pallas as pl
from jax.experimental.pallas import tpu as pltpu
from jax.sharding import PartitionSpec as P

MESH = pl.DeviceIdType.MESH
X, Y, Z = 4, 4, 16
HALF = Z // 2
PLANE = X * Y
FEAT, EIG, BLOCK = 192, 128, 128
PANEL = FEAT + EIG
PART = 12
PART_PAD = 16
REP = 16
COLS = 2 * PLANE
WIDE = COLS * BLOCK
CHUNK = 1024
PIECES = 4
ROOT = math.sqrt(2.0 * math.log2(math.e) / FEAT)
UNLISTED = -1024.0
OFFSETS = [0, HALF] + [o for s in range(1, HALF) for o in (HALF - s, s - HALF)]
SHIFTS = (0, -1, 1, 2)


def rem(a, b):
    return lax.rem(a, jnp.int32(b))


def place():
    blk, rep = lax.axis_index("blk"), lax.axis_index("rep")
    core, zl = rem(rep, 2), rep // 2
    zh, xy = rem(blk, 2), blk // 2
    return blk, rep, core, xy // Y, rem(xy, Y), zh * HALF + zl


def device(x, y, z, core):
    return {"blk": (x * Y + y) * 2 + z // HALF, "rep": rem(z, HALF) * 2 + core}


def copy_to(src, dst, send, recv, where):
    return pltpu.make_async_remote_copy(
        src_ref=src, dst_ref=dst, send_sem=send, recv_sem=recv, device_id=where, device_id_type=MESH
    )


def halves(value):
    high = value.astype(jnp.bfloat16)
    low = (value - high.astype(jnp.float32)).astype(jnp.bfloat16)
    return high, low


def dot(a, b):
    return jnp.dot(a, b, preferred_element_type=jnp.float32)


def half_norm(x):
    return 0.5 * jnp.sum(x * x, axis=0, keepdims=True)


def kernel(
    parts, vecs, lists, out,
    landed, far_lists, own_vecs, rows, cols, row_ops, col_ops, vec_ops, col_norms, row_lists, shifts,
    partial, up_in, down_in, up_sum, down_sum,
    part_send, part_recv, list_send, list_recv, z_send, z_recv, xy_send, xy_recv, pair_send, pair_recv,
    up_send, up_recv, down_send, down_recv,
):
    blk, rep, core, x, y, z = place()
    other = 1 - core
    here = device(x, y, z, core)
    up, down = device(x, y, rem(z + 1, Z), core), device(x, y, rem(z + Z - 1, Z), core)
    far = device(x, y, rem(z + HALF, Z), core)

    barrier = pltpu.get_barrier_semaphore()
    mates = [{"blk": blk, "rep": rem(rep + d, REP)} for d in range(1, REP)] + [up, down, far]
    mates += [device(rem(x + d, X), y, z, core) for d in (1, X - 1)]
    mates += [device(x, rem(y + d, Y), z, core) for d in (1, Y - 1)]
    for mate in mates:
        pl.semaphore_signal(barrier, inc=1, device_id=mate, device_id_type=MESH)
    own_vecs[...] = vecs[...].T
    cols[x * Y + y, core, FEAT:] = own_vecs[...]
    landed[rep] = parts[rep]
    up_in[0] = jnp.zeros_like(up_in[0])
    down_in[0] = jnp.zeros_like(down_in[0])
    pl.semaphore_wait(barrier, len(mates))

    for d in range(1, REP):
        to = rem(rep + d, REP)
        copy_to(parts.at[to], landed.at[rep], part_send, part_recv, {"blk": blk, "rep": to}).start()

    def spot(dx, dy):
        return rem(x + dx + X, X), rem(y + dy + Y, Y)

    def slot(dx, dy, k):
        return (SHIFTS.index(dx) * len(SHIFTS) + SHIFTS.index(dy)) * 2 + k

    def ready(phase, dx, dy, k):
        sx, sy = spot(dx, dy)
        q = slot(dx, dy, k)
        panel = cols.at[sx * Y + sy, core if k == 0 else other]
        if phase == 0:
            high, low = halves(panel[FEAT:])
            vec_ops[q * BLOCK : (q + 1) * BLOCK, :EIG] = high
            vec_ops[q * BLOCK : (q + 1) * BLOCK, EIG:] = low
            return
        coords = panel[:FEAT]
        high, low = halves(coords)
        lanes = slice(q * BLOCK, (q + 1) * BLOCK)
        col_ops[:FEAT, lanes] = high
        col_ops[FEAT : 2 * FEAT, lanes] = high
        col_ops[2 * FEAT : 3 * FEAT, lanes] = low
        col_ops[3 * FEAT :, lanes] = low
        col_norms[:, lanes] = jnp.broadcast_to(half_norm(coords), (8, BLOCK))

    def plane_steps(phase, base, size):
        half, quarter = size // 2, size // 4

        def region(turn, i, j, part, owner=core):
            sx, sy = spot(i, j) if turn == 0 else spot(j, i)
            start, count = base + turn * half, half
            if part is not None:
                start, count = start + part * quarter, quarter
            return cols.at[sx * Y + sy, owner, pl.ds(start, count)]

        def source(turn, i, j, ref):
            return own_vecs.at[pl.ds(turn * half, half)] if phase == 0 and (i, j) == (0, 0) else ref

        def send(turn, n, i, j, part, to):
            tx, ty = spot(*to) if turn == 0 else spot(to[1], to[0])
            ref = region(turn, i, j, part)
            sem = xy_recv.at[phase, turn * 20 + n]
            copy_to(source(turn, i, j, ref), ref, xy_send, sem, device(tx, ty, z, core)).start()

        def arrive(turn, n, i, j, part):
            ref = region(turn, i, j, part)
            copy_to(ref, ref, xy_send, xy_recv.at[phase, turn * 20 + n], here).wait_recv()

        def at(turn, i, j):
            dx, dy = (i, j) if turn == 0 else (j, i)
            return phase * COLS + turn * PLANE + slot(dx, dy, 0) // 2

        def share(turn, i, j):
            ref = region(turn, i, j, None)
            copy_to(source(turn, i, j, ref), ref, pair_send, pair_recv.at[at(turn, i, j)], device(x, y, z, other)).start()

        def take(i, j):
            for turn in range(2):
                a, b = (i, j) if turn == 0 else (j, i)
                ref = region(turn, a, b, None, other)
                copy_to(ref, ref, pair_send, pair_recv.at[at(turn, a, b)], here).wait_recv()
            ready(phase, i, j, 1)

        def spread(n, i):
            for turn in range(2):
                send(turn, 4 + 4 * n, i, 0, None, (0, 1))
                send(turn, 5 + 4 * n, i, 0, None, (0, -1))

        def relay(n, i):
            for turn in range(2):
                arrive(turn, 4 + 4 * n, i, -1, None)
                send(turn, 6 + 4 * n, i, -1, 0, (0, 1))
                share(turn, i, -1)
                arrive(turn, 5 + 4 * n, i, 1, None)
                send(turn, 7 + 4 * n, i, 1, 1, (0, -1))
                share(turn, i, 1)

        def finish(n, i):
            for turn in range(2):
                arrive(turn, 6 + 4 * n, i, 2, 0)
                arrive(turn, 7 + 4 * n, i, 2, 1)
                share(turn, i, 2)

        for turn in range(2):
            send(turn, 0, 0, 0, None, (1, 0))
            send(turn, 1, 0, 0, None, (-1, 0))
        spread(0, 0)
        for turn in range(2):
            share(turn, 0, 0)
        ready(phase, 0, 0, 0)
        yield
        for turn in range(2):
            arrive(turn, 0, -1, 0, None)
            send(turn, 2, -1, 0, 0, (1, 0))
            arrive(turn, 1, 1, 0, None)
            send(turn, 3, 1, 0, 1, (-1, 0))
        spread(1, -1)
        spread(2, 1)
        for turn in range(2):
            share(turn, -1, 0)
            share(turn, 1, 0)
        take(0, 0)
        yield
        relay(0, 0)
        for turn in range(2):
            arrive(turn, 2, 2, 0, 0)
            arrive(turn, 3, 2, 0, 1)
        spread(3, 2)
        for turn in range(2):
            share(turn, 2, 0)
        for a, b in ((0, 1), (0, -1), (1, 0), (-1, 0)):
            ready(phase, a, b, 0)
        yield
        relay(1, -1)
        relay(2, 1)
        for a in (-1, 1):
            for b in (-1, 1):
                ready(phase, a, b, 0)
        for a, b in ((0, 1), (0, -1), (1, 0), (-1, 0)):
            take(a, b)
        yield
        relay(3, 2)
        finish(0, 0)
        ready(phase, 0, 2, 0)
        ready(phase, 2, 0, 0)
        for a in (-1, 1):
            for b in (-1, 1):
                take(a, b)
        yield
        finish(1, -1)
        finish(2, 1)
        for a in (-1, 1):
            ready(phase, a, 2, 0)
            ready(phase, 2, a, 0)
        take(0, 2)
        take(2, 0)
        yield
        finish(3, 2)
        ready(phase, 2, 2, 0)
        for a in (-1, 1):
            take(a, 2)
            take(2, a)
        take(2, 2)

    def row_ready(offset):
        s = OFFSETS.index(offset)
        high, low = halves(rows[rem(z + offset + Z, Z)])
        both = jnp.concatenate([high.astype(jnp.float32), low.astype(jnp.float32)], axis=0)
        flipped = both.T.astype(jnp.bfloat16)
        place_at = slice(s % 2 * BLOCK, (s % 2 + 1) * BLOCK)
        row_ops[s // 2, place_at, : 2 * FEAT] = flipped
        row_ops[s // 2, place_at, 2 * FEAT :] = flipped

    def ring_steps():
        size = FEAT // PIECES

        def region(t, part):
            return rows.at[rem(z + t + Z, Z), pl.ds(part * size, size)]

        def send(t, way, part):
            ref = region(-t * way, part)
            sem = z_recv.at[(0 if way > 0 else HALF * PIECES) + t * PIECES + part]
            copy_to(ref, ref, z_send, sem, up if way > 0 else down).start()

        def arrive(t, way, part):
            ref = region(-t * way, part)
            sem = z_recv.at[(0 if way > 0 else HALF * PIECES) + (t - 1) * PIECES + part]
            copy_to(ref, ref, z_send, sem, here).wait_recv()

        def goes(t, way, part):
            return t < HALF - 1 or (part < PIECES // 2) == (way > 0)

        for part in range(PIECES):
            send(0, 1, part)
            send(0, -1, part)
        row_ready(0)
        yield
        for t in range(1, HALF):
            for part in range(PIECES):
                for way in (1, -1):
                    arrive(t, way, part)
                    if goes(t, way, part):
                        send(t, way, part)
            row_ready(t)
            row_ready(-t)
            yield
        for part in range(PIECES):
            arrive(HALF, 1 if part < PIECES // 2 else -1, part)
        row_ready(HALF)

    first = plane_steps(0, FEAT, EIG)
    next(first)
    copy_to(lists, far_lists, list_send, list_recv, far).start()
    next(first)
    next(first)
    gone = copy_to(parts.at[pl.ds(0, REP - 1)], landed.at[pl.ds(0, REP - 1)], part_send, part_recv, here)
    gone.wait_recv()
    me = x * Y + y
    for p in range(REP):
        piece = landed[p, :PART, :] * ROOT
        rows[z, p * PART : (p + 1) * PART] = piece
        cols[me, core, p * PART : (p + 1) * PART] = piece
    going = [ring_steps(), plane_steps(1, 0, FEAT), first]
    while going:
        going = [steps for steps in going if next(steps, "end") != "end"]

    copy_to(lists, far_lists, list_send, list_recv, here).wait()
    for s, offset in enumerate(OFFSETS):
        there = rem(z + offset + Z, Z)
        at = rem(there, HALF) * 2 + core
        row_lists[s : s + 1] = jnp.where(there // HALF == z // HALF, lists[at], far_lists[at])
    picked = row_lists[...]
    for dx in SHIFTS:
        for dy in SHIFTS:
            for k in range(2):
                sx, sy = spot(dx, dy)
                name = ((sx * Y + sy) * 2 + z // HALF) * REP + rem(z, HALF) * 2 + (core if k == 0 else other)
                found = jnp.max(jnp.where(picked == name, 1.0, 0.0), axis=1, keepdims=True)
                shift = jnp.where(found > 0.5, 0.0, UNLISTED)
                q = slot(dx, dy, k)
                lanes = slice(q * BLOCK, (q + 1) * BLOCK)
                shifts[:, lanes] = jnp.broadcast_to(shift, (2 * HALF, BLOCK)) - col_norms[:1, lanes]

    size = BLOCK // 2
    ways = (
        (1, up, up_in, up_sum, up_send, up_recv),
        (-1, down, down_in, down_sum, down_send, down_recv),
    )

    @pl.loop(0, HALF)
    def _(s):
        def chunk(n, total):
            c0 = pl.multiple_of(n * CHUNK, CHUNK)
            lanes = pl.ds(c0, CHUNK)
            power = dot(row_ops[s], col_ops[:, lanes])
            top = power[:BLOCK] + shifts[pl.ds(2 * s, 1), lanes]
            low = power[BLOCK:] + shifts[pl.ds(2 * s + 1, 1), lanes]
            high, low = halves(jnp.exp2(jnp.concatenate([top, low], axis=0)))
            ops = vec_ops[lanes]
            wide = dot(high, ops)
            return total + wide[:, :EIG] + wide[:, EIG:] + dot(low, ops[:, :EIG])

        zero = jnp.zeros((2 * BLOCK, EIG), jnp.float32)
        partial[s] = lax.fori_loop(0, WIDE // CHUNK, chunk, zero)

        @pl.when(s == 0)
        def _():
            copy_to(partial.at[0, pl.ds(BLOCK, size)], up_in.at[1], up_send, up_recv.at[1], up).start()
            copy_to(partial.at[0, pl.ds(BLOCK + size, size)], down_in.at[1], down_send, down_recv.at[1], down).start()

        @pl.when(s > 0)
        def _():
            for lead in range(2):
                for way, to, landing, sums, send, recv in ways:
                    start = (0 if way > 0 else BLOCK) + (lead if way > 0 else 1 - lead) * size
                    at = 2 * s + 1 - lead
                    ref = landing.at[at - 2]

                    def wait(ref=ref, send=send, sem=recv.at[at - 2]):
                        copy_to(ref, ref, send, sem, here).wait_recv()

                    if lead == 0:
                        wait()
                    else:
                        pl.when(s > 1)(wait)
                    sums[at] = partial[s, start : start + size] + landing[at - 2]
                    copy_to(sums.at[at], landing.at[at], send, recv.at[at], to).start()

    own_scale = jnp.exp2(-half_norm(rows[z]))
    for part in range(2):
        here_rows = slice(part * size, (part + 1) * size)
        total = partial[0, here_rows]
        for way, to, landing, sums, send, recv in ways:
            at = 2 * HALF - 1 - (part if way > 0 else 1 - part)
            ref = landing.at[at]
            copy_to(ref, ref, send, recv.at[at], here).wait_recv()
            total = total + landing[at]
        out[:, here_rows] = total.T * own_scale[:, here_rows]

    for way, to, landing, sums, send, recv in ways:
        fill = landing.at[pl.ds(1, 2 * HALF - 1)]
        copy_to(fill, fill, send, recv.at[0], here).wait_send()
    gone.wait_send()
    fill = rows.at[pl.ds(0, Z - 1)]
    copy_to(fill, fill, z_send, z_recv.at[0], here).wait_send()
    fill = cols.at[pl.ds(0, PLANE - 1), core]
    copy_to(fill, fill, xy_send, xy_recv.at[0, 0], here).wait_send()
    fill = cols.at[:, core]
    copy_to(fill, fill, pair_send, pair_recv.at[0], here).wait_send()


def shards(coords, eigvecs, nbr_list, nbr_count):
    f32, bf16 = jnp.float32, jnp.bfloat16
    vmem = pl.BlockSpec(memory_space=pltpu.VMEM)
    dma = pltpu.SemaphoreType.DMA

    parts = coords.reshape(PART, REP, BLOCK).transpose(1, 0, 2)
    parts = jnp.pad(parts, ((0, 0), (0, PART_PAD - PART), (0, 0)))
    slots = lax.broadcasted_iota(jnp.int32, nbr_list.shape, 1)
    lists = jnp.where(slots < nbr_count[:, None], nbr_list, -1).reshape(REP, 1, BLOCK)

    sums = pltpu.VMEM((2 * HALF, BLOCK // 2, EIG), f32)
    return pl.pallas_call(
        kernel,
        out_shape=jax.ShapeDtypeStruct((EIG, BLOCK), f32),
        in_specs=[vmem] * 3,
        out_specs=vmem,
        scratch_shapes=[
            pltpu.VMEM((REP, PART_PAD, BLOCK), f32),
            pltpu.VMEM((REP, 1, BLOCK), jnp.int32),
            pltpu.VMEM((BLOCK, EIG), f32),
            pltpu.VMEM((Z, FEAT, BLOCK), f32),
            pltpu.VMEM((PLANE, 2, PANEL, BLOCK), f32),
            pltpu.VMEM((HALF, 2 * BLOCK, 4 * FEAT), bf16),
            pltpu.VMEM((4 * FEAT, WIDE), bf16),
            pltpu.VMEM((WIDE, 2 * EIG), bf16),
            pltpu.VMEM((8, WIDE), f32),
            pltpu.VMEM((2 * HALF, BLOCK), jnp.int32),
            pltpu.VMEM((2 * HALF, WIDE), f32),
            pltpu.VMEM((HALF, 2 * BLOCK, EIG), f32),
            sums, sums, sums, sums,
            dma, dma, dma, dma,
            dma, dma((2 * HALF * PIECES,)),
            dma, dma((2, 40)),
            dma, dma((2 * COLS,)),
            dma, dma((2 * HALF,)),
            dma, dma((2 * HALF,)),
        ],
        compiler_params=pltpu.CompilerParams(collective_id=0, has_side_effects=True),
    )(parts, eigvecs, lists)


def solution(mesh):
    return jax.shard_map(
        shards,
        mesh=mesh,
        in_specs=(P("rep", "blk"), P(None, ("blk", "rep")), P("blk", None), P("blk")),
        out_specs=P(None, ("blk", "rep")),
        check_vma=False,
    )
```

time: 133 us -> 93 us (0.70); the launches traced: 130 us -> 92.7 us
  Pallas kernels: 124 us -> 88.9 us
  other arithmetic: 3.21 us -> 0.67 us
    pallas_call x3 -> x1, Pallas kernels: 124 us -> 88.9 us  [shards(): pl.pallas_call(kernel, out_shape=jax.ShapeDtypeStruct((EIG, BLOCK), f32),...]
    select_n x2 -> x1, other arithmetic: 2.17 us -> 0.67 us  [shards(): jnp.where(slots < nbr_count[:, None], nbr_list, -1).reshape(REP, 1, BLOCK)]
where the time goes in v2:
time: 93 us; the launch traced here: 92.7 us
  Pallas kernels  88.9 us (96%)
  local copies, waits for them, and re-layouts  3.13 us (3%)
    pallas_call x1, Pallas kernels, shards(): pl.pallas_call(kernel, out_shape=jax.ShapeDtypeStruct((EIG, BLOCK), f32),...  88.9 us
    unnamed x6, local copies, waits for them, and re-layouts  2.44 us

profile of v2, /device:TPU:6, one launch (start us, length us, event | category | flops | bytes accessed | tf_op | source)
XLA Modules:
  0.0 92.7 jit_solution(8779466179697103880)
XLA Ops:
  0.0 0.9 %copy.6 = f32[2,8,16,128]{3,2,1,0:T(8,128)S(1)} copy(f32[2,8,16,128]{3,1,2,0:T(8,128)} %bitcast.9) | data formatting | bytes 262144
  1.0 0.0 copy-start
  1.0 0.0 copy-start.1
  1.0 0.6 pad.4.parts
  1.7 0.0 copy-done
  1.7 0.0 copy-done.1
  1.7 0.7 fusion
  2.4 88.9 %shard_map.46 = f32[128,128]{1,0:T(8,128)} custom-call(f32[16,16,128]{2,1,0:T(8,128)} %pad.4.parts, f32[128,128]{1,0:T(8,128)} %vecs.1, s32[16,1,128]{2,1,0:T(1,128)} %bitcast.10), custom_call_target="tpu_custom_call" | custom-call | tf_op jit(solution)/shard_map/pallas_call | solution.py:395
  91.2 1.5 %copy.10 = f32[128,128]{1,0:T(8,128)} copy(f32[128,128]{1,0:T(8,128)} %shard_map.46) | data formatting | bytes 131072
  (2 shorter events, 0.0 us)
Async XLA Ops:
  1.0 0.7 copy-start
  1.0 0.7 copy-start.1

commit v3 on v2

v3 whole, which is shorter than its diff:
```python
import math

import jax
import jax.numpy as jnp
from jax import lax
from jax.experimental import pallas as pl
from jax.experimental.pallas import tpu as pltpu
from jax.sharding import PartitionSpec as P

MESH = pl.DeviceIdType.MESH
X, Y, Z = 4, 4, 16
HALF = Z // 2
PLANE = X * Y
FEAT, EIG, BLOCK = 192, 128, 128
PANEL = FEAT + EIG
PART = 12
PART_PAD = 16
REP = 16
COLS = 2 * PLANE
WIDE = COLS * BLOCK
PACK = HALF * PART
PIECES = 4
WAIT = 3
ROOT = math.sqrt(2.0 * math.log2(math.e) / FEAT)
UNLISTED = -1024.0
PLACES = [
    (0, 0), (0, 1), (0, -1), (1, 0), (-1, 0), (1, 1), (1, -1), (-1, 1),
    (-1, -1), (0, 2), (2, 0), (1, 2), (-1, 2), (2, 1), (2, -1), (2, 2),
]


def rem(a, b):
    return lax.rem(a, jnp.int32(b))


def place():
    blk, rep = lax.axis_index("blk"), lax.axis_index("rep")
    core, zl = rem(rep, 2), rep // 2
    zh, xy = rem(blk, 2), blk // 2
    return blk, rep, core, xy // Y, rem(xy, Y), zh * HALF + zl


def device(x, y, z, core):
    return {"blk": (x * Y + y) * 2 + z // HALF, "rep": rem(z, HALF) * 2 + core}


def copy_to(src, dst, send, recv, where):
    return pltpu.make_async_remote_copy(
        src_ref=src, dst_ref=dst, send_sem=send, recv_sem=recv, device_id=where, device_id_type=MESH
    )


def halves(value):
    high = value.astype(jnp.bfloat16)
    low = (value - high.astype(jnp.float32)).astype(jnp.bfloat16)
    return high, low


def dot(a, b):
    return jnp.dot(a, b, preferred_element_type=jnp.float32)


def half_norm(x):
    return 0.5 * jnp.sum(x * x, axis=0, keepdims=True)


def kernel(
    coords, vecs, names, counts, out,
    parts, packs, landed, lists, far_lists, rows, cols, row_ops, col_ops, vec_ops, row_lists, shifts,
    partial, up_in, down_in, up_sum, down_sum,
    part_send, part_recv, list_send, list_recv, z_send, z_recv, xy_send, xy_recv, pair_send, pair_recv,
    up_send, up_recv, down_send, down_recv, swap_send, swap_recv,
):
    blk, rep, core, x, y, z = place()
    other = 1 - core
    here = device(x, y, z, core)
    up, down = device(x, y, rem(z + 1, Z), core), device(x, y, rem(z + Z - 1, Z), core)
    far = device(x, y, rem(z + HALF, Z), core)

    barrier = pltpu.get_barrier_semaphore()
    mates = [{"blk": blk, "rep": rem(rep + d, REP)} for d in range(1, REP)] + [up, down, far]
    mates += [device(rem(x + d, X), y, z, core) for d in (1, X - 1)]
    mates += [device(x, rem(y + d, Y), z, core) for d in (1, Y - 1)]
    for mate in mates:
        pl.semaphore_signal(barrier, inc=1, device_id=mate, device_id_type=MESH)
    for p in range(REP):
        piece = coords[:, p * BLOCK : (p + 1) * BLOCK] * ROOT
        parts[p, :PART] = piece
        packs[p % 2, p // 2 * PART : (p // 2 + 1) * PART] = piece
        parts[p, PART:] = jnp.zeros((PART_PAD - PART, BLOCK), jnp.float32)
        used = lax.broadcasted_iota(jnp.int32, (1, BLOCK), 1) < counts[p]
        lists[p] = jnp.where(used, names[p : p + 1], -1)
    cols[x * Y + y, core, FEAT:] = vecs[...].T
    landed[rep] = parts[rep]
    rows[z, core] = packs[core]
    up_in[0] = jnp.zeros_like(up_in[0])
    down_in[0] = jnp.zeros_like(down_in[0])
    pl.semaphore_wait(barrier, len(mates))

    for d in range(1, REP):
        to = rem(rep + d, REP)
        copy_to(parts.at[to], landed.at[rep], part_send, part_recv, {"blk": blk, "rep": to}).start()
    copy_to(lists, far_lists, list_send, list_recv, far).start()

    def swap(landing):
        return copy_to(packs.at[other], landing, swap_send, swap_recv, device(x, y, z, other))

    swap(rows.at[z, core]).start()

    def spot(dx, dy):
        return rem(x + dx + X, X), rem(y + dy + Y, Y)

    def slot(dx, dy, k):
        return PLACES.index((dx, dy)) * 2 + k

    def ready(dx, dy, k):
        sx, sy = spot(dx, dy)
        q = slot(dx, dy, k)
        panel = cols.at[sx * Y + sy, core if k == 0 else other]
        high, low = halves(panel[FEAT:])
        vec_ops[q * BLOCK : (q + 1) * BLOCK, :EIG] = high
        vec_ops[q * BLOCK : (q + 1) * BLOCK, EIG:] = low
        block = panel[:FEAT]
        high, low = halves(block)
        lanes = slice(q * BLOCK, (q + 1) * BLOCK)
        col_ops[:FEAT, lanes] = high
        col_ops[FEAT : 2 * FEAT, lanes] = high
        col_ops[2 * FEAT : 3 * FEAT, lanes] = low
        col_ops[3 * FEAT :, lanes] = low
        name = ((sx * Y + sy) * 2 + z // HALF) * REP + rem(z, HALF) * 2 + (core if k == 0 else other)
        found = jnp.max(jnp.where(row_lists[...] == name, 1.0, 0.0), axis=-1, keepdims=True)
        shift = jnp.where(found > 0.5, 0.0, UNLISTED)
        shifts[:, :, :, lanes] = jnp.broadcast_to(shift, (HALF, 2, 1, BLOCK)) - half_norm(block)

    def pair_of(there):
        offset = rem(there - z + Z, Z)
        return jnp.where(offset >= HALF, offset - HALF, rem(HALF - offset + HALF, HALF)), offset // HALF

    def note_lists():
        copy_to(lists, far_lists, list_send, list_recv, here).wait()
        for there in range(Z):
            pair, side = pair_of(jnp.int32(there))
            at = there % HALF * 2 + core
            row_lists[pair, side] = jnp.where(there // HALF == z // HALF, lists[at], far_lists[at])

    def products(s):
        power = dot(row_ops[s].reshape(2 * BLOCK, 4 * FEAT), col_ops[...])
        power = [power[side * BLOCK : (side + 1) * BLOCK] + shifts[s, side] for side in range(2)]
        high, low = halves(jnp.exp2(jnp.concatenate(power, axis=0)))
        wide = dot(high, vec_ops[...])
        return wide[:, :EIG] + wide[:, EIG:] + dot(low, vec_ops[:, :EIG])

    def plane_steps():
        half, quarter = PANEL // 2, PANEL // 4

        def region(turn, i, j, part, owner=core):
            sx, sy = spot(i, j) if turn == 0 else spot(j, i)
            start, count = turn * half, half
            if part is not None:
                start, count = start + part * quarter, quarter
            return cols.at[sx * Y + sy, owner, pl.ds(start, count)]

        def send(turn, n, i, j, part, to):
            tx, ty = spot(*to) if turn == 0 else spot(to[1], to[0])
            ref = region(turn, i, j, part)
            sem = xy_recv.at[turn * 20 + n]
            copy_to(ref, ref, xy_send, sem, device(tx, ty, z, core)).start()

        def arrive(turn, n, i, j, part):
            ref = region(turn, i, j, part)
            copy_to(ref, ref, xy_send, xy_recv.at[turn * 20 + n], here).wait_recv()

        def at(turn, i, j):
            dx, dy = (i, j) if turn == 0 else (j, i)
            return turn * PLANE + slot(dx, dy, 0) // 2

        def share(turn, i, j):
            ref = region(turn, i, j, None)
            copy_to(ref, ref, pair_send, pair_recv.at[at(turn, i, j)], device(x, y, z, other)).start()

        def take(i, j):
            for turn in range(2):
                a, b = (i, j) if turn == 0 else (j, i)
                ref = region(turn, a, b, None, other)
                copy_to(ref, ref, pair_send, pair_recv.at[at(turn, a, b)], here).wait_recv()
            ready(i, j, 1)

        def spread(n, i):
            for turn in range(2):
                send(turn, 4 + 4 * n, i, 0, None, (0, 1))
                send(turn, 5 + 4 * n, i, 0, None, (0, -1))

        def relay(n, i):
            for turn in range(2):
                arrive(turn, 4 + 4 * n, i, -1, None)
                send(turn, 6 + 4 * n, i, -1, 0, (0, 1))
                share(turn, i, -1)
                arrive(turn, 5 + 4 * n, i, 1, None)
                send(turn, 7 + 4 * n, i, 1, 1, (0, -1))
                share(turn, i, 1)

        def finish(n, i):
            for turn in range(2):
                arrive(turn, 6 + 4 * n, i, 2, 0)
                arrive(turn, 7 + 4 * n, i, 2, 1)
                share(turn, i, 2)

        for turn in range(2):
            send(turn, 0, 0, 0, None, (1, 0))
            send(turn, 1, 0, 0, None, (-1, 0))
        spread(0, 0)
        for turn in range(2):
            share(turn, 0, 0)
        note_lists()
        ready(0, 0, 0)
        yield
        for turn in range(2):
            arrive(turn, 0, -1, 0, None)
            send(turn, 2, -1, 0, 0, (1, 0))
            arrive(turn, 1, 1, 0, None)
            send(turn, 3, 1, 0, 1, (-1, 0))
        spread(1, -1)
        spread(2, 1)
        for turn in range(2):
            share(turn, -1, 0)
            share(turn, 1, 0)
        take(0, 0)
        yield
        relay(0, 0)
        for turn in range(2):
            arrive(turn, 2, 2, 0, 0)
            arrive(turn, 3, 2, 0, 1)
        spread(3, 2)
        for turn in range(2):
            share(turn, 2, 0)
        for a, b in ((0, 1), (0, -1), (1, 0), (-1, 0)):
            ready(a, b, 0)
        yield
        relay(1, -1)
        relay(2, 1)
        for a in (-1, 1):
            for b in (-1, 1):
                ready(a, b, 0)
        for a, b in ((0, 1), (0, -1), (1, 0), (-1, 0)):
            take(a, b)
        yield
        relay(3, 2)
        finish(0, 0)
        ready(0, 2, 0)
        ready(2, 0, 0)
        for a in (-1, 1):
            for b in (-1, 1):
                take(a, b)
        yield
        finish(1, -1)
        finish(2, 1)
        for a in (-1, 1):
            ready(a, 2, 0)
            ready(2, a, 0)
        take(0, 2)
        take(2, 0)
        yield
        finish(3, 2)
        ready(2, 2, 0)
        for a in (-1, 1):
            take(a, 2)
            take(2, a)
        take(2, 2)

    def rows_ready():
        for there in range(Z):
            start = there % HALF * PART
            pieces = [
                rows[there // HALF * HALF + n // 2, n % 2, start : start + PART] for n in range(REP)
            ]
            high, low = halves(jnp.concatenate(pieces, axis=0))
            both = jnp.concatenate([high.astype(jnp.float32), low.astype(jnp.float32)], axis=0)
            flipped = both.T.astype(jnp.bfloat16)
            pair, side = pair_of(jnp.int32(there))
            row_ops[pair, side, :, : 2 * FEAT] = flipped
            row_ops[pair, side, :, 2 * FEAT :] = flipped

    def ring_steps():
        size = PACK // 2

        def region(t, part):
            owner = core if part < PIECES // 2 else other
            return rows.at[rem(z + t + Z, Z), owner, pl.ds(part % 2 * size, size)]

        def send(t, way, part):
            ref = region(-t * way, part)
            sem = z_recv.at[(0 if way > 0 else HALF * PIECES) + t * PIECES + part]
            copy_to(ref, ref, z_send, sem, up if way > 0 else down).start()

        def arrive(t, way, part):
            ref = region(-t * way, part)
            sem = z_recv.at[(0 if way > 0 else HALF * PIECES) + (t - 1) * PIECES + part]
            copy_to(ref, ref, z_send, sem, here).wait_recv()

        def goes(t, way, part):
            return t < HALF - 1 or (part < PIECES // 2) == (way > 0)

        for part in range(PIECES):
            if part == PIECES // 2:
                swap(rows.at[z, other]).wait()
            send(0, 1, part)
            send(0, -1, part)
        yield
        for t in range(1, HALF):
            for part in range(PIECES):
                for way in (1, -1):
                    arrive(t, way, part)
                    if goes(t, way, part):
                        send(t, way, part)
            yield
        for part in range(PIECES):
            arrive(HALF, 1 if part < PIECES // 2 else -1, part)

    def own_block():
        gone.wait_recv()
        for p in range(REP):
            cols[x * Y + y, core, p * PART : (p + 1) * PART] = landed[p, :PART, :]

    gone = copy_to(parts.at[pl.ds(0, REP - 1)], landed.at[pl.ds(0, REP - 1)], part_send, part_recv, here)
    ring, plane = ring_steps(), plane_steps()
    for step in range(WAIT):
        next(ring)
    own_block()
    next(plane)
    going = [ring, plane]
    while going:
        going = [steps for steps in going if next(steps, "end") != "end"]
    rows_ready()

    size = BLOCK // 2
    ways = (
        (1, up, up_in, up_sum, up_send, up_recv),
        (-1, down, down_in, down_sum, down_send, down_recv),
    )

    @pl.loop(0, HALF)
    def _(s):
        partial[s] = products(s)

        @pl.when(s == 0)
        def _():
            copy_to(partial.at[0, pl.ds(BLOCK, size)], up_in.at[1], up_send, up_recv.at[1], up).start()
            copy_to(partial.at[0, pl.ds(BLOCK + size, size)], down_in.at[1], down_send, down_recv.at[1], down).start()

        @pl.when(s > 0)
        def _():
            for lead in range(2):
                for way, to, landing, sums, send, recv in ways:
                    start = (0 if way > 0 else BLOCK) + (lead if way > 0 else 1 - lead) * size
                    at = 2 * s + 1 - lead
                    ref = landing.at[at - 2]

                    def wait(ref=ref, send=send, sem=recv.at[at - 2]):
                        copy_to(ref, ref, send, sem, here).wait_recv()

                    if lead == 0:
                        wait()
                    else:
                        pl.when(s > 1)(wait)
                    sums[at] = partial[s, start : start + size] + landing[at - 2]
                    copy_to(sums.at[at], landing.at[at], send, recv.at[at], to).start()

    own_scale = jnp.exp2(-half_norm(cols[x * Y + y, core, :FEAT]))
    for part in range(2):
        here_rows = slice(part * size, (part + 1) * size)
        total = partial[0, here_rows]
        for way, to, landing, sums, send, recv in ways:
            at = 2 * HALF - 1 - (part if way > 0 else 1 - part)
            ref = landing.at[at]
            copy_to(ref, ref, send, recv.at[at], here).wait_recv()
            total = total + landing[at]
        out[:, here_rows] = total.T * own_scale[:, here_rows]

    for way, to, landing, sums, send, recv in ways:
        fill = landing.at[pl.ds(1, 2 * HALF - 1)]
        copy_to(fill, fill, send, recv.at[0], here).wait_send()
    gone.wait_send()
    fill = rows.at[pl.ds(0, Z - 1)]
    copy_to(fill, fill, z_send, z_recv.at[0], here).wait_send()
    fill = cols.at[pl.ds(0, PLANE - 1), core]
    copy_to(fill, fill, xy_send, xy_recv.at[0], here).wait_send()
    fill = cols.at[:, core]
    copy_to(fill, fill, pair_send, pair_recv.at[0], here).wait_send()


def shards(coords, eigvecs, nbr_list, nbr_count):
    f32, bf16 = jnp.float32, jnp.bfloat16
    vmem = pl.BlockSpec(memory_space=pltpu.VMEM)
    dma = pltpu.SemaphoreType.DMA

    sums = pltpu.VMEM((2 * HALF, BLOCK // 2, EIG), f32)
    return pl.pallas_call(
        kernel,
        out_shape=jax.ShapeDtypeStruct((EIG, BLOCK), f32),
        in_specs=[vmem] * 3 + [pl.BlockSpec(memory_space=pltpu.SMEM)],
        out_specs=vmem,
        scratch_shapes=[
            pltpu.VMEM((REP, PART_PAD, BLOCK), f32),
            pltpu.VMEM((2, PACK, BLOCK), f32),
            pltpu.VMEM((REP, PART_PAD, BLOCK), f32),
            pltpu.VMEM((REP, 1, BLOCK), jnp.int32),
            pltpu.VMEM((REP, 1, BLOCK), jnp.int32),
            pltpu.VMEM((Z, 2, PACK, BLOCK), f32),
            pltpu.VMEM((PLANE, 2, PANEL, BLOCK), f32),
            pltpu.VMEM((HALF, 2, BLOCK, 4 * FEAT), bf16),
            pltpu.VMEM((4 * FEAT, WIDE), bf16),
            pltpu.VMEM((WIDE, 2 * EIG), bf16),
            pltpu.VMEM((HALF, 2, 1, BLOCK), jnp.int32),
            pltpu.VMEM((HALF, 2, 1, WIDE), f32),
            pltpu.VMEM((HALF, 2 * BLOCK, EIG), f32),
            sums, sums, sums, sums,
            dma, dma, dma, dma,
            dma, dma((2 * HALF * PIECES,)),
            dma, dma((40,)),
            dma, dma((COLS,)),
            dma, dma((2 * HALF,)),
            dma, dma((2 * HALF,)),
            dma, dma,
        ],
        compiler_params=pltpu.CompilerParams(collective_id=0, has_side_effects=True),
    )(coords, eigvecs, nbr_list, nbr_count)


def solution(mesh):
    return jax.shard_map(
        shards,
        mesh=mesh,
        in_specs=(P("rep", "blk"), P(None, ("blk", "rep")), P("blk", None), P("blk")),
        out_specs=P(None, ("blk", "rep")),
        check_vma=False,
    )
```

time: 93 us -> 87.4 us (0.940)
  Pallas kernels: 88.9 us -> 85.4 us
  local copies, waits for them, and re-layouts: 3.13 us -> 1.47 us
    pallas_call x1, Pallas kernels: 88.9 us -> 85.4 us  [shards(): pl.pallas_call(kernel, out_shape=jax.ShapeDtypeStruct((EIG, BLOCK), f32),...]
    unnamed x6 -> x1, local copies, waits for them, and re-layouts: 2.44 us -> 1.47 us
where the time goes in v3:
time: 87.4 us; the launch traced here: 86.8 us
  Pallas kernels  85.4 us (98%)
  local copies, waits for them, and re-layouts  1.47 us (2%)
    pallas_call x1, Pallas kernels, shards(): pl.pallas_call(kernel, out_shape=jax.ShapeDtypeStruct((EIG, BLOCK), f32),...  85.4 us

profile of v3, /device:TPU:6, one launch (start us, length us, event | category | flops | bytes accessed | tf_op | source)
XLA Modules:
  0.0 86.8 jit_solution(7552720725371661266)
XLA Ops:
  0.0 85.4 %shard_map.46 = f32[128,128]{1,0:T(8,128)} custom-call(f32[12,2048]{1,0:T(8,128)} %coords.1, f32[128,128]{1,0:T(8,128)} %vecs.1, s32[16,128]{1,0:T(8,128)} %names.1, s32[16]{0:T(128)} %counts.1), custom_call_target="tpu_custom_call" | custom-call | tf_op jit(solution)/shard_map/pallas_call | solution.py:397
  85.4 1.5 %copy.6 = f32[128,128]{1,0:T(8,128)} copy(f32[128,128]{1,0:T(8,128)} %shard_map.46) | data formatting | bytes 131072

commit v4 on v3

--- a/solution.py
+++ b/solution.py
@@ -14,7 +14,6 @@
 FEAT, EIG, BLOCK = 192, 128, 128
 PANEL = FEAT + EIG
 PART = 12
-PART_PAD = 16
 REP = 16
 COLS = 2 * PLANE
 WIDE = COLS * BLOCK
@@ -65,7 +64,8 @@
 
 
 def kernel(
-    coords, vecs, names, counts, out,
+    coords_in, vecs_in, names_in, counts, out,
+    coords, vecs, names, in_sem,
     parts, packs, landed, lists, far_lists, rows, cols, row_ops, col_ops, vec_ops, row_lists, shifts,
     partial, up_in, down_in, up_sum, down_sum,
     part_send, part_recv, list_send, list_recv, z_send, z_recv, xy_send, xy_recv, pair_send, pair_recv,
@@ -83,11 +83,18 @@
     mates += [device(x, rem(y + d, Y), z, core) for d in (1, Y - 1)]
     for mate in mates:
         pl.semaphore_signal(barrier, inc=1, device_id=mate, device_id_type=MESH)
+    loads = [
+        pltpu.make_async_copy(src, dst, in_sem.at[n])
+        for n, (src, dst) in enumerate(((coords_in, coords), (names_in, names), (vecs_in, vecs)))
+    ]
+    for load in loads:
+        load.start()
+    for load in loads:
+        load.wait()
     for p in range(REP):
         piece = coords[:, p * BLOCK : (p + 1) * BLOCK] * ROOT
         parts[p, :PART] = piece
         packs[p % 2, p // 2 * PART : (p // 2 + 1) * PART] = piece
-        parts[p, PART:] = jnp.zeros((PART_PAD - PART, BLOCK), jnp.float32)
         used = lax.broadcasted_iota(jnp.int32, (1, BLOCK), 1) < counts[p]
         lists[p] = jnp.where(used, names[p : p + 1], -1)
     cols[x * Y + y, core, FEAT:] = vecs[...].T
@@ -97,7 +104,7 @@
     down_in[0] = jnp.zeros_like(down_in[0])
     pl.semaphore_wait(barrier, len(mates))
 
-    for d in range(1, REP):
+    for d in sorted(range(1, REP), key=lambda d: abs(d - HALF)):
         to = rem(rep + d, REP)
         copy_to(parts.at[to], landed.at[rep], part_send, part_recv, {"blk": blk, "rep": to}).start()
     copy_to(lists, far_lists, list_send, list_recv, far).start()
@@ -281,11 +288,12 @@
             row_ops[pair, side, :, 2 * FEAT :] = flipped
 
     def ring_steps():
-        size = PACK // 2
+        count = PIECES // 2
+        size = PACK // count
 
         def region(t, part):
             owner = core if part < PIECES // 2 else other
-            return rows.at[rem(z + t + Z, Z), owner, pl.ds(part % 2 * size, size)]
+            return rows.at[rem(z + t + Z, Z), owner, pl.ds(part % count * size, size)]
 
         def send(t, way, part):
             ref = region(-t * way, part)
@@ -397,12 +405,16 @@
     return pl.pallas_call(
         kernel,
         out_shape=jax.ShapeDtypeStruct((EIG, BLOCK), f32),
-        in_specs=[vmem] * 3 + [pl.BlockSpec(memory_space=pltpu.SMEM)],
+        in_specs=[pl.BlockSpec(memory_space=pl.ANY)] * 3 + [pl.BlockSpec(memory_space=pltpu.SMEM)],
         out_specs=vmem,
         scratch_shapes=[
-            pltpu.VMEM((REP, PART_PAD, BLOCK), f32),
+            pltpu.VMEM((PART, REP * BLOCK), f32),
+            pltpu.VMEM((EIG, BLOCK), f32),
+            pltpu.VMEM((REP, BLOCK), jnp.int32),
+            dma((3,)),
+            pltpu.VMEM((REP, PART, BLOCK), f32),
             pltpu.VMEM((2, PACK, BLOCK), f32),
-            pltpu.VMEM((REP, PART_PAD, BLOCK), f32),
+            pltpu.VMEM((REP, PART, BLOCK), f32),
             pltpu.VMEM((REP, 1, BLOCK), jnp.int32),
             pltpu.VMEM((REP, 1, BLOCK), jnp.int32),
             pltpu.VMEM((Z, 2, PACK, BLOCK), f32),

time: 87.4 us -> 85.9 us (0.983)
  Pallas kernels: 85.4 us -> 84.1 us
    pallas_call x1, Pallas kernels: 85.4 us -> 84.1 us  [shards(): pl.pallas_call(kernel, out_shape=jax.ShapeDtypeStruct((EIG, BLOCK), f32),...]
where the time goes in v4:
time: 85.9 us; the launch traced here: 85.6 us
  Pallas kernels  84.1 us (98%)
  local copies, waits for them, and re-layouts  1.47 us (2%)
    pallas_call x1, Pallas kernels, shards(): pl.pallas_call(kernel, out_shape=jax.ShapeDtypeStruct((EIG, BLOCK), f32),...  84.1 us

profile of v4, /device:TPU:6, one launch (start us, length us, event | category | flops | bytes accessed | tf_op | source)
XLA Modules:
  0.0 85.6 jit_solution(6747148455883217761)
XLA Ops:
  0.0 84.1 %shard_map.46 = f32[128,128]{1,0:T(8,128)} custom-call(f32[12,2048]{1,0:T(8,128)} %coords_in.1, f32[128,128]{1,0:T(8,128)} %vecs_in.1, s32[16,128]{1,0:T(8,128)} %names_in.1, s32[16]{0:T(128)} %counts.1), custom_call_target="tpu_custom_call" | custom-call | tf_op jit(solution)/shard_map/pallas_call | solution.py:405
  84.1 1.5 %copy.6 = f32[128,128]{1,0:T(8,128)} copy(f32[128,128]{1,0:T(8,128)} %shard_map.46) | data formatting | bytes 131072

commit v5 on v4

--- a/solution.py
+++ b/solution.py
@@ -19,7 +19,7 @@
 WIDE = COLS * BLOCK
 PACK = HALF * PART
 PIECES = 4
-WAIT = 3
+WAIT = 2
 ROOT = math.sqrt(2.0 * math.log2(math.e) / FEAT)
 UNLISTED = -1024.0
 PLACES = [

time: 85.9 us -> 85.8 us (level)
  no operation moved by 1% of the time
where the time goes in v5:
time: 85.8 us; the launch traced here: 84.8 us
  Pallas kernels  83.4 us (97%)
  local copies, waits for them, and re-layouts  1.47 us (2%)
    pallas_call x1, Pallas kernels, shards(): pl.pallas_call(kernel, out_shape=jax.ShapeDtypeStruct((EIG, BLOCK), f32),...  83.4 us

profile of v5, /device:TPU:6, one launch (start us, length us, event | category | flops | bytes accessed | tf_op | source)
XLA Modules:
  0.0 84.8 jit_solution(1045604658296577742)
XLA Ops:
  0.0 83.4 %shard_map.46 = f32[128,128]{1,0:T(8,128)} custom-call(f32[12,2048]{1,0:T(8,128)} %coords_in.1, f32[128,128]{1,0:T(8,128)} %vecs_in.1, s32[16,128]{1,0:T(8,128)} %names_in.1, s32[16]{0:T(128)} %counts.1), custom_call_target="tpu_custom_call" | custom-call | tf_op jit(solution)/shard_map/pallas_call | solution.py:405
  83.4 1.5 %copy.6 = f32[128,128]{1,0:T(8,128)} copy(f32[128,128]{1,0:T(8,128)} %shard_map.46) | data formatting | bytes 131072
